TPU v7x, 512 devices: a whole 4x8x8 slice. The times are simulated.
512 devices in a mesh: req: 32 (over z_hi, x, core), seq: 16 (over z_lo, y).
Axes of the slice: x: 4, y: 8, z: 8 (z_hi: 4, z_lo: 2; z = z_hi * 2 + z_lo), core: 2. Of those that a mesh axis runs over, the one named last changes fastest.
Arguments:
- layer_input: bfloat16 [32, 256, 2048], P('req', 'seq'), may hold values from -3 to 3
- queries: bfloat16 [32, 256, 4096], P('req', 'seq'), may hold values from -4.5 to 4.5
- fresh_kv: bfloat16 [32, 256, 1024], P('req', 'seq'), may hold values from -4.5 to 4.5
- cache_kv: bfloat16 [32, 1792, 1024], P('req', 'seq'), may hold values from -4.5 to 4.5
- cached_len: int32 [32], P('req'), may hold values from 2 to 1792, as said below
- out_weight: bfloat16 [4096, 2048], P('seq', 'req'), may hold values from -0.09375 to 0.09375
- norm_gain: float32 [2048], replicated, may hold values from 0.5 to 1.5
- routes: int32 [32, 256, 8], P('req', 'seq'), may hold values from 0 to 127, all different within a row; in each aligned block of 16 rows (0 to 15, 16 to 31, ..., all dimensions but the last counted through in order) at most 2 rows name the same one
- route_gates: float32 [32, 256, 8], P('req', 'seq'), may hold values from 0.2 to 1
- w_gate_up: bfloat16 [512, 2048, 384], P(('req', 'seq')), may hold values from -0.125 to 0.125
- w_down: bfloat16 [512, 192, 2048], P(('req', 'seq')), may hold values from -0.21875 to 0.21875
Outputs:
- output: bfloat16 [32, 256, 2048], P('req', 'seq')
Inputs may be any that keep to these rules, and one draw needn't show every extreme that they name: Request r has cached_len[r] valid cached rows; some request has exactly 1792. `routes`: each token names 8 different experts; among the 16 tokens of one device (aligned blocks), no expert is named more than 2 times.
All inputs are finite; a program needn't handle non-finite values.
Results may differ from a plain program's by a relative error of at most 0.03.
Values may be sent and summed in bfloat16 or wider, within the bound.
A program may use at most 64 MiB of HBM per device.

v0:
```python
import math

import jax
import jax.numpy as jnp
from jax import lax
from jax.sharding import PartitionSpec as P

QH = 32
KVH = 4
HD = 128
EXPERTS = 128
TOP = 8
CAP = 2


neg_large = -1e30
epsilon = 1e-06


def local(
    layer_input,
    queries,
    fresh_kv,
    cache_kv,
    cached_len,
    out_weight,
    norm_gain,
    routes,
    route_gates,
    w_gate_up,
    w_down,
):
    new_dev = queries.shape[1]
    cache_dev = cache_kv.shape[1]
    query_width = queries.shape[2]
    kv_width = fresh_kv.shape[2] // 2
    seq_count = lax.axis_size("seq")
    req_count = lax.axis_size("req")
    group_size = QH // KVH
    scale = 1.0 / math.sqrt(HD)
    block_rows = cache_dev + new_dev
    length = cached_len[0]
    query_pos = lax.axis_index("seq") * new_dev + jnp.arange(new_dev, dtype=jnp.int32)
    grouped = queries[0].reshape(new_dev, KVH, group_size, HD)
    key_block = jnp.concatenate([cache_kv[0], fresh_kv[0]], 0)
    shard_rows = lax.all_gather(key_block, "seq", axis=0, tiled=True)
    row_count = shard_rows.shape[0]
    row_index = jnp.arange(row_count, dtype=jnp.int32)
    source_dev = row_index // block_rows
    within = row_index % block_rows
    in_cache = within < cache_dev
    cache_live = source_dev * cache_dev + within < length
    fresh_live = (source_dev * new_dev + within - cache_dev)[None, :] <= query_pos[:, None]
    visible = jnp.where(in_cache[None, :], cache_live[None, :], fresh_live)
    running_max = jnp.full((new_dev, KVH, group_size), neg_large, jnp.float32)
    key_part = shard_rows[:, :kv_width].reshape(row_count, KVH, HD)
    value_part = shard_rows[:, kv_width:].reshape(row_count, KVH, HD)
    scores = (
        jnp.einsum("ngqc,pgc->ngqp", grouped, key_part, preferred_element_type=jnp.float32) * scale
    )
    mask = visible[:, None, None, :]
    scores = jnp.where(mask, scores, neg_large)
    new_max = jnp.maximum(running_max, jnp.max(scores, axis=-1))
    weights = jnp.where(mask, jnp.exp(scores - new_max[..., None]), 0.0)
    denominator = jnp.sum(weights, axis=-1)
    mixed_values = jnp.einsum(
        "ngqp,pgc->ngqc",
        weights.astype(jnp.bfloat16),
        value_part,
        preferred_element_type=jnp.float32,
    )
    numerator = mixed_values
    running_max, denominator, numerator = (new_max, denominator, numerator)
    attended = (
        (numerator / denominator[..., None]).reshape(new_dev, query_width).astype(jnp.bfloat16)
    )
    by_heads = lax.all_to_all(attended, "seq", split_axis=1, concat_axis=0, tiled=True)
    proj_full = lax.all_gather(out_weight, "req", axis=1, tiled=True)
    projected = lax.psum_scatter(
        jnp.dot(by_heads, proj_full, preferred_element_type=jnp.float32).astype(jnp.bfloat16),
        "seq",
        scatter_dimension=0,
        tiled=True,
    ).astype(jnp.float32)
    residual = (layer_input[0].astype(jnp.float32) + projected).astype(jnp.bfloat16)
    residual_f = residual.astype(jnp.float32)
    normed = (
        residual_f
        * lax.rsqrt(jnp.mean(residual_f * residual_f, axis=-1, keepdims=True) + epsilon)
        * norm_gain
    ).astype(jnp.bfloat16)
    owned_count = EXPERTS // req_count
    slab_count = w_gate_up.shape[0]
    split_count = seq_count * slab_count // owned_count
    hidden_part = w_down.shape[1]
    model_width = normed.shape[1]
    pair_count = new_dev * TOP
    chosen = routes[0].reshape(pair_count)
    onehot = (chosen[:, None] == jnp.arange(EXPERTS, dtype=jnp.int32)[None, :]).astype(jnp.int32)
    earlier = jnp.cumsum(onehot, axis=0) - onehot
    slot_at = jnp.sum(earlier * onehot, axis=1)
    target = chosen * CAP + slot_at
    placed = (target[:, None] == jnp.arange(EXPERTS * CAP, dtype=jnp.int32)[None, :]).astype(
        jnp.float32
    )
    placed_rows = placed.reshape(new_dev, TOP, EXPERTS * CAP)
    picker = jnp.sum(placed_rows, axis=1).astype(jnp.bfloat16)
    outgoing = lax.dot_general(
        picker, normed, (((0,), (0,)), ((), ())), preferred_element_type=jnp.float32
    )
    outgoing = outgoing.astype(jnp.bfloat16).reshape(req_count, owned_count, CAP, model_width)
    combine_rows = jnp.sum(placed_rows * route_gates[0][:, :, None], axis=1)
    arrived_req = lax.all_to_all(outgoing, "req", split_axis=0, concat_axis=0, tiled=True)
    spread_out = jnp.broadcast_to(
        arrived_req[:, :, None], (req_count, owned_count, split_count, CAP, model_width)
    )
    arrived = lax.all_to_all(
        spread_out.reshape(req_count, seq_count, slab_count, CAP, model_width),
        "seq",
        split_axis=1,
        concat_axis=1,
        tiled=True,
    )
    token_rows = arrived[:, :, 0].reshape(req_count * seq_count * CAP, model_width)
    both = jnp.dot(token_rows, w_gate_up[0], preferred_element_type=jnp.float32)
    hidden = (jax.nn.silu(both[:, :hidden_part]) * both[:, hidden_part:]).astype(jnp.bfloat16)
    part_out = jnp.dot(hidden, w_down[0], preferred_element_type=jnp.float32).astype(jnp.bfloat16)
    produced_list = [part_out.reshape(req_count, seq_count, CAP, model_width)]
    produced = jnp.stack(produced_list, axis=2)
    returned = lax.all_to_all(produced, "seq", split_axis=1, concat_axis=1, tiled=True)
    grouped_parts = returned.reshape(req_count, owned_count, split_count, CAP, model_width).astype(
        jnp.float32
    )
    result = lax.all_to_all(
        jnp.sum(grouped_parts, axis=2).astype(jnp.bfloat16),
        "req",
        split_axis=0,
        concat_axis=0,
        tiled=True,
    )
    expert_rows = result.reshape(EXPERTS * CAP, model_width).astype(jnp.float32)
    mixture = jnp.dot(combine_rows, expert_rows, precision=lax.Precision.HIGHEST)
    output = (residual_f + mixture).astype(jnp.bfloat16)
    return output[None]


def solution(mesh):
    return jax.shard_map(
        local,
        mesh=mesh,
        in_specs=(
            P("req", "seq", None),
            P("req", "seq", None),
            P("req", "seq", None),
            P("req", "seq", None),
            P("req"),
            P("seq", "req"),
            P(),
            P("req", "seq", None),
            P("req", "seq", None),
            P(("req", "seq"), None, None),
            P(("req", "seq"), None, None),
        ),
        out_specs=P("req", "seq", None),
        check_vma=False,
    )
```

profile of v0, /device:TPU:6, one launch (start us, length us, event | category | flops | bytes accessed | tf_op | source)
XLA Modules:
  0.0 570.4 jit_solution(9128146810409177649)
XLA Ops:
  6.5 1.2 copy.99
  12.1 93.5 %all-gather.3.cloned.1.call-done = bf16[2048,1024]{0,1:T(8,128)(2,1)} async-done(((bf16[128,1024]{0,1:T(8,128)(2,1)}), bf16[2048,1024]{0,1:T(8,128)(2,1)}) %all-gather.3.cloned.1.call-update) | async-done | bytes 4194320 | tf_op jit(solution)/shard_map/all_gather | solution.py:46
  105.6 2.8 fusion.51
  109.4 1.2 fusion.1
  112.5 5.9 %all-to-all-start = ((bf16[16,16,256]{2,0,1:T(8,128)(2,1)}), bf16[16,16,256]{2,0,1:T(8,128)(2,1)S(1)}, u32[]{:S(2)}, u32[]{:S(2)}) async-start(bf16[16,16,256]{2,0,1:T(8,128)(2,1)} %copy.105), calls=%async_computation | async-start | bytes 262144 | tf_op jit(solution)/shard_map/all_to_all | solution.py:77
  118.4 46.4 %all-gather.5.cloned.1.call-done = bf16[256,2048]{0,1:T(8,128)(2,1)} async-done(((bf16[256,64]{0,1:T(8,128)(2,1)}), bf16[256,2048]{0,1:T(8,128)(2,1)}) %all-gather.5.cloned.1.call-update) | async-done | bytes 1048592 | tf_op jit(solution)/shard_map/all_gather | solution.py:78
  164.8 2.7 convolution_convert_fusion.1
  168.7 71.7 %reduce-scatter.2.cloned.1.call-done = bf16[16,2048]{1,0:T(8,128)(2,1)} async-done(((bf16[256,2048]{1,0:T(8,128)(2,1)}), bf16[16,2048]{1,0:T(8,128)(2,1)}) %reduce-scatter.2.cloned.1.call-update) | async-done | bytes 65552 | tf_op jit(solution)/shard_map/reduce_scatter | solution.py:79
  241.3 1.3 convolution_convert_fusion.2
  242.6 1.5 reshape.147
  244.1 38.3 %all_to_all.36 = bf16[32,4,2,2048]{3,2,1,0:T(2,128)(2,1)S(1)} all-to-all(bf16[32,4,2,2048]{3,2,1,0:T(2,128)(2,1)} %reshape.147), channel_id=1, replica_groups=mesh['req'=32,'seq'=16] {'req'}, dimensions={0} | all-to-all | bytes 2097152 | tf_op jit(solution)/shard_map/all_to_all | solution.py:113
  283.3 5.4 broadcast_in_dim.64
  288.7 96.4 %all_to_all.37 = bf16[32,16,1,2,2048]{4,3,0,2,1:T(2,128)(2,1)S(1)} all-to-all(bf16[32,16,1,2,2048]{4,3,0,2,1:T(2,128)(2,1)} %bitcast.81), channel_id=1, replica_groups=mesh['req'=32,'seq'=16] {'seq'}, dimensions={1} | all-to-all | bytes 8388608 | tf_op jit(solution)/shard_map/all_to_all | solution.py:117
  385.1 6.5 %copy.111 = bf16[32,16,1,2,2048]{4,3,1,0,2:T(2,128)(2,1)} copy(bf16[32,16,1,2,2048]{4,3,0,2,1:T(2,128)(2,1)S(1)} %all_to_all.37) | data formatting | bytes 8388608 | tf_op jit(solution)/shard_map/all_to_all | solution.py:117
  391.5 7.2 %reshape_squeeze.8 = bf16[1024,2048]{1,0:T(8,128)(2,1)} reshape(bf16[32,16,1,2,2048]{4,3,1,0,2:T(2,128)(2,1)} %copy.111) | data formatting | bytes 8388608 | tf_op jit(solution)/shard_map/reshape;squeeze | solution.py:124
  398.8 4.1 fusion.8
  402.9 3.2 convolution_convert_fusion
  406.1 7.6 %stack_reshape.3 = bf16[32,16,1,2,2048]{4,3,1,0,2:T(2,128)(2,1)} reshape(bf16[1024,2048]{1,0:T(8,128)(2,1)} %convolution_convert_fusion) | data formatting | bytes 8388608 | tf_op jit(solution)/shard_map/stack;reshape | solution.py:129
  413.7 6.0 %copy.112 = bf16[32,16,1,2,2048]{4,3,0,2,1:T(2,128)(2,1)S(1)} copy(bf16[32,16,1,2,2048]{4,3,1,0,2:T(2,128)(2,1)} %stack_reshape.3) | data formatting | bytes 8388608 | tf_op jit(solution)/shard_map/stack;reshape | solution.py:129
  419.8 97.6 %all_to_all.38 = bf16[32,16,1,2,2048]{4,3,0,2,1:T(2,128)(2,1)} all-to-all(bf16[32,16,1,2,2048]{4,3,0,2,1:T(2,128)(2,1)S(1)} %copy.112), channel_id=1, replica_groups=mesh['req'=32,'seq'=16] {'seq'}, dimensions={1} | all-to-all | bytes 8388608 | tf_op jit(solution)/shard_map/all_to_all | solution.py:130
  517.4 7.2 %bitcast_reduce_fusion = bf16[32,4,2,2048]{3,2,0,1:T(2,128)(2,1)S(1)} fusion(bf16[32,4,4,2,2048]{4,3,0,2,1:T(2,128)(2,1)} %bitcast.82), kind=kLoop, calls=%fused_computation | loop fusion | flops 1572864 | bytes 5242880 | tf_op jit(solution)/shard_map/reduce_sum | solution.py:135
  525.7 35.6 %all_to_all.39 = bf16[32,4,2,2048]{3,2,1,0:T(2,128)(2,1)} all-to-all(bf16[32,4,2,2048]{3,2,1,0:T(2,128)(2,1)S(1)} %copy.113), channel_id=1, replica_groups=mesh['req'=32,'seq'=16] {'req'}, dimensions={0} | all-to-all | bytes 2097152 | tf_op jit(solution)/shard_map/all_to_all | solution.py:134
  561.3 1.5 reshape.150
  562.7 1.2 fusion.4
  (49 shorter events, 10.5 us)
Async XLA Ops:
  6.5 392.2 %copy-start = (bf16[1,2048,384]{2,1,0:T(8,128)(2,1)S(1)}, bf16[1,2048,384]{2,1,0:T(8,128)(2,1)}, u32[]{:S(2)}) copy-start(bf16[1,2048,384]{2,1,0:T(8,128)(2,1)} %param.20) | copy-start | bytes 4718596
  6.5 99.1 %all-gather.3.cloned.1.call-start = ((), (), s32[]{:S(2)}) async-start(), calls=%async_computation.6 | async-start | bytes 4456448 | tf_op jit(solution)/shard_map/all_gather | solution.py:46
  9.6 155.2 %all-gather.5.cloned.1.call-start = ((), (), s32[]{:S(2)}) async-start(), calls=%async_computation.7 | async-start | bytes 1081344 | tf_op jit(solution)/shard_map/all_gather | solution.py:78
  111.6 55.9 %copy-start.3 = (s32[1,16,8]{1,2,0:T(8,128)S(1)}, s32[1,16,8]{1,2,0:T(8,128)}, u32[]{:S(2)}) copy-start(s32[1,16,8]{1,2,0:T(8,128)} %param.18) | copy-start | bytes 1540
  111.7 56.8 %copy-start.5 = (f32[1,16,8]{1,2,0:T(8,128)S(1)}, f32[1,16,8]{1,2,0:T(8,128)}, u32[]{:S(2)}) copy-start(f32[1,16,8]{1,2,0:T(8,128)} %param.19) | copy-start | bytes 1540
  111.7 128.6 %copy-start.1 = (bf16[1,16,2048]{2,1,0:T(8,128)(2,1)S(1)}, bf16[1,16,2048]{2,1,0:T(8,128)(2,1)}, u32[]{:S(2)}) copy-start(bf16[1,16,2048]{2,1,0:T(8,128)(2,1)} %param.11) | copy-start | bytes 196612
  111.7 129.6 %copy-start.4 = (f32[2048]{0:T(1024)S(1)}, f32[2048]{0:T(1024)}, u32[]{:S(2)}) copy-start(f32[2048]{0:T(1024)} %param.17) | copy-start | bytes 24580
  112.5 52.4 %all-to-all-start = ((bf16[16,16,256]{2,0,1:T(8,128)(2,1)}), bf16[16,16,256]{2,0,1:T(8,128)(2,1)S(1)}, u32[]{:S(2)}, u32[]{:S(2)}) async-start(bf16[16,16,256]{2,0,1:T(8,128)(2,1)} %copy.105), calls=%async_computation | async-start | bytes 262144 | tf_op jit(solution)/shard_map/all_to_all | solution.py:77
  118.4 121.9 %reduce-scatter.2.cloned.1.call-start = ((), (), s32[]{:S(2)}) async-start(), calls=%async_computation.8 | async-start | bytes 1114112 | tf_op jit(solution)/shard_map/reduce_scatter | solution.py:79
  398.7 4.1 copy-start.6
  524.6 38.2 %copy-start.2 = (bf16[16,2048]{1,0:T(8,128)(2,1)S(1)}, bf16[16,2048]{1,0:T(8,128)(2,1)}, u32[]{:S(2)}) copy-start(bf16[16,2048]{1,0:T(8,128)(2,1)} %reduce-scatter.2.cloned.1.call-done) | copy-start | bytes 196612
Sparse Core Ops, SparseCore 0:
  9.7 95.8 all-gather.2
  108.7 56.0 all-gather.4
  167.7 72.5 reduce-scatter.1
where the time goes:
time: 572 us; the launch traced here: 570 us
  blocking collectives  268 us (47%)
  waiting for transfers between devices  212 us (37%)
  local copies, waits for them, and re-layouts  44.8 us (8%)
  matrix products  14.5 us (3%)
  between operations  14 us (2%)
  other arithmetic  10.9 us (2%)
  starting transfers between devices  5.99 us (1%)
    all_to_all x1, blocking collectives, local(): lax.all_to_all(produced, 'seq', split_axis=1, concat_axis=1, tiled=True)  97.6 us
    all_to_all x1, blocking collectives, local(): lax.all_to_all(spread_out.reshape(req_count, seq_count, slab_count, CAP,...  96.4 us
    all_gather x1, waiting for transfers between devices, local(): shard_rows = lax.all_gather(key_block, 'seq', axis=0, tiled=True)  93.5 us
    reduce_scatter x1, waiting for transfers between devices, local(): lax.psum_scatter(jnp.dot(by_heads, proj_full, preferred_element_type=jnp....  71.7 us
    all_gather x1, waiting for transfers between devices, local(): proj_full = lax.all_gather(out_weight, 'req', axis=1, tiled=True)  46.4 us
    all_to_all x1, blocking collectives, local(): lax.all_to_all(outgoing, 'req', split_axis=0, concat_axis=0, tiled=True)  38.3 us
    all_to_all x1, blocking collectives, local(): lax.all_to_all(jnp.sum(grouped_parts, axis=2).astype(jnp.bfloat16), 'req'...  35.6 us
    another operation x2, local copies, waits for them, and re-layouts, local(): produced = jnp.stack(produced_list, axis=2)  13.7 us
  transfers between devices with their start and end apart: 4, of which 3 were waited for; matrix products, arithmetic and copies ran while one was open for 2% of the time, Pallas kernels for 0%

commit v1 on v0

v1 whole, which is shorter than its diff:
```python
import math

import jax
import jax.numpy as jnp
from jax import lax
from jax.experimental import pallas as pl
from jax.experimental.pallas import tpu as pltpu
from jax.sharding import PartitionSpec as P

MESH = pl.DeviceIdType.MESH
BF = jnp.bfloat16
F32 = jnp.float32
NEG = -1e30
EPS = 1e-06
D = 2048
HD = 128
NT = (((1,), (1,)), ((), ()))


def coords():
    req, seq = lax.axis_index("req"), lax.axis_index("seq")
    z = (req // 8) * 2 + seq // 8
    return (req // 2) % 4, seq % 8, z, req % 2


def device(x, y, z, c):
    return ((z // 2) * 8 + x * 2 + c, (z % 2) * 8 + y)


def remote(src, dst, send, recv, dev):
    return pltpu.make_async_remote_copy(
        src_ref=src, dst_ref=dst, send_sem=send, recv_sem=recv, device_id=dev, device_id_type=MESH
    )


def greet(devs):
    barrier = pltpu.get_barrier_semaphore()
    for dev in devs:
        pl.semaphore_signal(barrier, inc=1, device_id=dev, device_id_type=MESH)
    pl.semaphore_wait(barrier, len(devs))


def attention_kernel(
    len_ref, kv_ref, q_ref, wt_ref, x_ref, gain_ref, res_ref, normed_ref,
    kbuf, vbuf, qbuf, wbuf, att, pbuf, rbuf,
    own_sem, kv_send, kv_recv, w_send, w_recv, sib_send, sib_recv, p_send, p_recv,
):
    req, seq = lax.axis_index("req"), lax.axis_index("seq")
    m, c = req // 2, req % 2
    peers = [(req, lax.rem(seq + i, 16)) for i in range(1, 16)]
    chips = [(lax.rem(m + i, 16) * 2 + c, seq) for i in range(1, 16)]
    sibling = (m * 2 + 1 - c, seq)
    greet(peers + chips + [sibling])

    def piece(part, dst_seq, src_seq, i):
        rows = pl.ds(pl.multiple_of(src_seq * 128, 128), 128)
        head = dst_seq // 4
        if part == 0:
            cols = pl.ds(pl.multiple_of(head * HD, HD), HD)
            return kv_ref.at[:, cols], kbuf.at[rows, :]
        if part == 1:
            cols = pl.ds(pl.multiple_of(512 + head * HD, HD), HD)
            return kv_ref.at[:, cols], vbuf.at[rows, :]
        rows = pl.ds(pl.multiple_of(src_seq * 16, 16), 16)
        cols = pl.ds(pl.multiple_of(dst_seq * 256, 256), 256)
        return q_ref.at[:, cols], qbuf.at[rows, :]

    def kv_copy(part, i):
        dst_seq = lax.rem(seq + i, 16)
        src, dst = piece(part, dst_seq, seq, i)
        return remote(src, dst, kv_send.at[part, i], kv_recv.at[part, i], (req, dst_seq))

    def w_copy(i):
        return remote(
            wt_ref, wbuf.at[m, c], w_send.at[i], w_recv.at[i], (lax.rem(m + i, 16) * 2 + c, seq)
        )

    def start(i, _):
        for part in range(3):
            kv_copy(part, i).start()
        w_copy(i).start()
        return 0

    lax.fori_loop(1, 16, start, 0)
    own = []
    for part in range(3):
        src, dst = piece(part, seq, seq, 0)
        own.append(pltpu.make_async_copy(src, dst, own_sem.at[part]))
    own.append(pltpu.make_async_copy(wt_ref, wbuf.at[m, c], own_sem.at[3]))
    for copy in own:
        copy.start()
    for copy in own:
        copy.wait()

    def kv_wait(i, _):
        for part in range(3):
            kv_copy(part, i).wait()
        return 0

    def w_wait(i, _):
        w_copy(i).wait()
        return 0

    lax.fori_loop(1, 16, w_wait, 0)
    sib = remote(wbuf.at[:, c], wbuf.at[:, c], sib_send, sib_recv, sibling)
    sib.start()
    lax.fori_loop(1, 16, kv_wait, 0)

    length = len_ref[0]
    scale = 1.0 / math.sqrt(HD)
    for head in range(2):

        def tile(i, _):
            rows = pl.ds(pl.multiple_of(i * 64, 64), 64)
            q = qbuf[rows, head * HD : (head + 1) * HD]
            s = lax.dot_general(q, kbuf[...], NT, preferred_element_type=F32) * scale
            col = lax.broadcasted_iota(jnp.int32, (64, D), 1)
            tok = lax.broadcasted_iota(jnp.int32, (64, D), 0) + i * 64
            src, within = col >> 7, col & 127
            behind = jnp.where(
                within < 112, src * 112 + within - length, src * 16 + within - 113 - tok
            )
            seen = behind < 0
            s = jnp.where(seen, s, NEG)
            w = jnp.where(seen, jnp.exp(s - jnp.max(s, axis=-1, keepdims=True)), 0.0)
            total = jnp.sum(w, axis=-1, keepdims=True)
            mixed = jnp.dot(w.astype(BF), vbuf[...], preferred_element_type=F32)
            att[rows, head * HD : (head + 1) * HD] = (mixed / total).astype(BF)
            return 0

        lax.fori_loop(0, 4, tile, 0)

    sib.wait()

    def project(i, _):
        w = wbuf[pl.ds(i * 4, 4)].reshape(512, 256)
        cols = pl.ds(pl.multiple_of(i * 512, 512), 512)
        pbuf[:, cols] = lax.dot_general(att[...], w, NT, preferred_element_type=F32).astype(BF)
        return 0

    lax.fori_loop(0, 4, project, 0)

    def p_copy(i):
        dst_seq = lax.rem(seq + i, 16)
        rows = pl.ds(pl.multiple_of(dst_seq * 16, 16), 16)
        return remote(pbuf.at[rows, :], rbuf.at[i], p_send.at[i], p_recv.at[i], (req, dst_seq))

    def p_start(i, _):
        p_copy(i).start()
        return 0

    def p_wait(i, _):
        p_copy(i).wait()
        return 0

    lax.fori_loop(1, 16, p_start, 0)
    rbuf[0] = pbuf[pl.ds(pl.multiple_of(seq * 16, 16), 16), :]
    lax.fori_loop(1, 16, p_wait, 0)
    projected = lax.fori_loop(
        0, 16, lambda i, acc: acc + rbuf[i].astype(F32), jnp.zeros((16, D), F32)
    )
    residual = (x_ref[...].astype(F32) + projected).astype(BF)
    res_ref[...] = residual
    r = residual.astype(F32)
    mean = jnp.mean(r * r, axis=-1, keepdims=True)
    normed_ref[...] = (r * lax.rsqrt(mean + EPS) * gain_ref[...]).astype(BF)


def attention(cached_len, kv, q, wt, x, gain):
    vm = pl.BlockSpec(memory_space=pltpu.VMEM)
    dma = pltpu.SemaphoreType.DMA
    return pl.pallas_call(
        attention_kernel,
        name="attention",
        out_shape=[jax.ShapeDtypeStruct((16, D), BF)] * 2,
        in_specs=[pl.BlockSpec(memory_space=pltpu.SMEM)] + [vm] * 5,
        out_specs=[vm] * 2,
        scratch_shapes=[
            pltpu.VMEM((2048, HD), BF),
            pltpu.VMEM((2048, HD), BF),
            pltpu.VMEM((256, 256), BF),
            pltpu.VMEM((16, 2, 64, 256), BF),
            pltpu.VMEM((256, 256), BF),
            pltpu.VMEM((256, D), BF),
            pltpu.VMEM((16, 16, D), BF),
            dma((4,)),
            dma((3, 16)), dma((3, 16)),
            dma((16,)), dma((16,)),
            dma, dma,
            dma((16,)), dma((16,)),
        ],
        compiler_params=pltpu.CompilerParams(collective_id=0, has_side_effects=True),
    )(cached_len, kv, q, wt, x, gain)


def experts_kernel(
    normed_ref, res_ref, rt_ref, gt_ref, wg_ref, wd_ref, out_ref,
    tok, comb, xs, xr, po, pr, sl, rl, sr, rr, fs, fr,
    z_send, z_recv, y_send, y_recv, x_send, x_recv, b_send, b_recv, r_send, r_recv, f_send, f_recv,
):
    x, y, z, c = coords()
    q = x * 2 + c
    right, left = device(x, lax.rem(y + 1, 8), z, c), device(x, lax.rem(y + 7, 8), z, c)

    def at_q(j):
        n = lax.rem(q + j, 8)
        return device(n // 2, y, z, lax.rem(n, 2))

    zs = [device(x, y, lax.rem(z + i, 8), c) for i in range(1, 8)]
    greet(zs + [right, left] + [at_q(j) for j in range(1, 8)])

    own_rows = pl.ds(pl.multiple_of(z * 16, 16), 16)

    def z_copy(i):
        dev = device(x, y, lax.rem(z + i, 8), c)
        return remote(normed_ref, tok.at[0, own_rows], z_send.at[i], z_recv.at[i], dev)

    for i in range(1, 8):
        z_copy(i).start()
    tok[0, own_rows] = normed_ref[...]
    for i in range(1, 8):
        z_copy(i).wait()

    def half(h):
        return pl.ds(h * 1024, 1024)

    def y_copy(way, t, h):
        if way == 0:
            a, b, dev = t, t + 1, right
        else:
            a, b, dev = (8 - t) % 8, 7 - t, left
        return remote(
            tok.at[a, :, half(h)], tok.at[b, :, half(h)], y_send.at[way, t, h], y_recv.at[way, t, h], dev
        )

    def steps(t):
        return [(0, 0), (1, 0), (0, 1), (1, 1)] if t < 3 else [(0, 0), (1, 1)]

    def x_copy(o, j):
        return remote(xs.at[o, j], xr.at[o, j], x_send.at[o, j], x_recv.at[o, j], at_q(j))

    def b_copy(o, j):
        return remote(po.at[o, j], pr.at[o, j], b_send.at[o, j], b_recv.at[o, j], at_q(8 - j))

    seq, zhi = (z % 2) * 8 + y, z // 2

    def select(o):
        y0 = lax.rem(y + 8 - o, 8)
        rt, gt = rt_ref[y0], gt_ref[y0]
        row = lax.broadcasted_iota(jnp.int32, (128, 128), 0)
        col = lax.broadcasted_iota(jnp.int32, (128, 128), 1)
        expert = 4 * (zhi * 8 + ((q + (row >> 4)) & 7)) + seq // 4
        same = ((row >> 1) & 7) == (col >> 4)
        match = jnp.zeros((128, 128), F32)
        gate = jnp.zeros((128, 128), F32)
        for k in range(8):
            hit = same & (rt[k : k + 1, :] == expert)
            match = jnp.where(hit, 1.0, match)
            gate = jnp.where(hit, gt[k : k + 1, :], gate)
        before = jnp.where(row < col, 1.0, 0.0).astype(BF)
        rank = jnp.dot(match.astype(BF), before, preferred_element_type=F32)
        pick = jnp.where(rank == (row & 1).astype(F32), match, 0.0)
        comb[o] = (pick * gate).T.astype(BF)
        pick = pick.astype(BF)

        def tile(n, _):
            cols = pl.ds(pl.multiple_of(n * 512, 512), 512)
            rows = jnp.dot(pick, tok[o, :, cols], preferred_element_type=F32).astype(BF)
            xs[o, :, :, cols] = rows.reshape(8, 16, 512)
            xr[o, 0, :, cols] = rows[:16]
            return 0

        lax.fori_loop(0, 4, tile, 0)

        def send(j, _):
            x_copy(o, j).start()
            return 0

        lax.fori_loop(1, 8, send, 0)

    def feed(o):
        def arrive(j, _):
            x_copy(o, j).wait_recv()
            return 0

        lax.fori_loop(1, 8, arrive, 0)
        both = jnp.dot(xr[o].reshape(128, D), wg_ref[...], preferred_element_type=F32)
        g, u = both[:, :192], both[:, 192:]
        hidden = (g / (1.0 + jnp.exp(-g)) * u).astype(BF)

        def tile(n, _):
            cols = pl.ds(pl.multiple_of(n * 512, 512), 512)
            rows = jnp.dot(hidden, wd_ref[:, cols], preferred_element_type=F32).astype(BF)
            po[o, :, :, cols] = rows.reshape(8, 16, 512)
            pr[o, 0, :, cols] = rows[:16]
            return 0

        lax.fori_loop(0, 4, tile, 0)

        def send(j, _):
            b_copy(o, j).start()
            return 0

        lax.fori_loop(1, 8, send, 0)

    def returned(o):
        def arrive(j, _):
            b_copy(o, j).wait_recv()
            return 0

        lax.fori_loop(1, 8, arrive, 0)

    def combined(o, cols):
        rows = pr[o, :, :, cols].reshape(128, cols.size)
        return jnp.dot(comb[o], rows, preferred_element_type=F32)

    def pair(f, o):
        def one(i, _):
            f(jnp.where(i == 0, o, 8 - o))
            return 0

        lax.fori_loop(0, 2, one, 0)

    for way, h in steps(0):
        y_copy(way, 0, h).start()
    select(0)
    for t in range(1, 4):
        for way, h in steps(t - 1):
            y_copy(way, t - 1, h).wait_recv()
            if (way, h) in steps(t):
                y_copy(way, t, h).start()
        pair(select, t)
        if t == 1:
            feed(0)
        else:
            pair(feed, t - 1)
    for way, h in steps(3):
        y_copy(way, 3, h).wait_recv()
    select(4)
    pair(feed, 3)
    feed(4)

    def r_copy(way, t, h):
        src, dst, dev = (sl, rl, left) if way == 0 else (sr, rr, right)
        return remote(
            src.at[t, :, half(h)], dst.at[t, :, half(h)], r_send.at[way, t, h], r_recv.at[way, t, h], dev
        )

    def r_steps(t):
        return [(0, 0), (1, 1)] if t == 0 else [(0, 0), (1, 1), (0, 1), (1, 0)]

    for t in range(4):
        for o in {4 - t, 4 + t}:
            returned(o)
        for way, h in r_steps(t):
            o = 4 - t if way == 0 else 4 + t
            came = t > 0 and (way, h) in r_steps(t - 1)
            if came:
                r_copy(way, t - 1, h).wait_recv()
            src, dst = (sl, rl) if way == 0 else (sr, rr)

            def tile(n, _):
                cols = pl.ds(pl.multiple_of(h * 1024 + n * 512, 512), 512)
                part = combined(o, cols)
                if came:
                    part = part + dst[t - 1, :, cols].astype(F32)
                src[t, :, cols] = part.astype(BF)
                return 0

            lax.fori_loop(0, 2, tile, 0)
            r_copy(way, t, h).start()

    returned(0)
    for way, h in r_steps(3):
        r_copy(way, 3, h).wait_recv()

    def total(n, _):
        cols = pl.ds(pl.multiple_of(n * 512, 512), 512)
        part = combined(0, cols) + rl[3, :, cols].astype(F32) + rr[3, :, cols].astype(F32)
        fs[:, cols] = part.astype(BF)
        return 0

    lax.fori_loop(0, 4, total, 0)

    def f_copy(i):
        n = lax.rem(z + i, 8)
        rows = pl.ds(pl.multiple_of(n * 16, 16), 16)
        return remote(fs.at[rows, :], fr.at[i], f_send.at[i], f_recv.at[i], device(x, y, n, c))

    for i in range(1, 8):
        f_copy(i).start()
    acc = res_ref[...].astype(F32) + fs[own_rows, :].astype(F32)
    for i in range(1, 8):
        f_copy(i).wait()
        acc = acc + fr[i].astype(F32)
    out_ref[...] = acc.astype(BF)

    for t in range(4):
        for way, h in steps(t):
            y_copy(way, t, h).wait_send()
        for way, h in r_steps(t):
            r_copy(way, t, h).wait_send()

    def sent(o, _):
        def one(j, _):
            x_copy(o, j).wait_send()
            b_copy(o, j).wait_send()
            return 0

        return lax.fori_loop(1, 8, one, 0)

    lax.fori_loop(0, 8, sent, 0)


def experts(normed, residual, rt, gt, wg, wd):
    vm = pl.BlockSpec(memory_space=pltpu.VMEM)
    dma = pltpu.SemaphoreType.DMA
    big = pltpu.VMEM((8, 8, 16, D), BF)
    hop = pltpu.VMEM((4, 128, D), BF)
    return pl.pallas_call(
        experts_kernel,
        name="experts",
        out_shape=jax.ShapeDtypeStruct((16, D), BF),
        in_specs=[vm] * 6,
        out_specs=vm,
        scratch_shapes=[
            pltpu.VMEM((8, 128, D), BF),
            pltpu.VMEM((8, 128, 128), BF),
            big, big, big, big,
            hop, hop, hop, hop,
            pltpu.VMEM((128, D), BF),
            pltpu.VMEM((8, 16, D), BF),
            dma((8,)), dma((8,)),
            dma((2, 4, 2)), dma((2, 4, 2)),
            dma((8, 8)), dma((8, 8)),
            dma((8, 8)), dma((8, 8)),
            dma((2, 4, 2)), dma((2, 4, 2)),
            dma((8,)), dma((8,)),
        ],
        compiler_params=pltpu.CompilerParams(
            collective_id=1, has_side_effects=True, vmem_limit_bytes=56 * 1024 * 1024
        ),
    )(normed, residual, rt, gt, wg, wd)


def local(
    layer_input, queries, fresh_kv, cache_kv, cached_len, out_weight, norm_gain,
    routes, route_gates, w_gate_up, w_down,
):
    x, y, z, c = coords()

    def table(a):
        whole = lax.all_gather(a[0].T.reshape(1, 128), ("req", "seq"), axis=0, tiled=True)
        whole = whole.reshape(4, 8, 2, 8, 128)
        mine = lax.dynamic_slice_in_dim(whole, x * 2 + c, 1, axis=1)[:, 0]
        return mine.reshape(4, 2, 8, 8, 16).transpose(2, 3, 0, 1, 4).reshape(8, 8, 128)

    rt, gt = table(routes), table(route_gates)
    kv = jnp.concatenate([cache_kv[0], fresh_kv[0]], 0)
    residual, normed = attention(
        cached_len, kv, queries[0], out_weight.T, layer_input[0], norm_gain[None]
    )
    return experts(normed, residual, rt, gt, w_gate_up[0], w_down[0])[None]


def solution(mesh):
    return jax.shard_map(
        local,
        mesh=mesh,
        in_specs=(
            P("req", "seq", None),
            P("req", "seq", None),
            P("req", "seq", None),
            P("req", "seq", None),
            P("req"),
            P("seq", "req"),
            P(),
            P("req", "seq", None),
            P("req", "seq", None),
            P(("req", "seq"), None, None),
            P(("req", "seq"), None, None),
        ),
        out_specs=P("req", "seq", None),
        check_vma=False,
    )
```

time: 572 us -> 2730 us (4.77)
  blocking collectives: 268 us -> 2240 us
  Pallas kernels: 0 us -> 480 us
  waiting for transfers between devices: 212 us -> 0 us
  local copies, waits for them, and re-layouts: 44.8 us -> 5.55 us
    all_gather x0 -> x2, blocking collectives: none -> 2240 us  [table(): lax.all_gather(a[0].T.reshape(1, 128), ('req', 'seq'), axis=0, tiled=True)]
    pallas_call x0 -> x2, Pallas kernels: none -> 480 us  [the longest x1 288 us: attention(): pl.pallas_call(attention_kernel, name='attention', out_shape=[jax.ShapeDt...]
    all_to_all x4 -> x0, blocking collectives: 268 us -> none  [the longest x1 97.6 us: local(): lax.all_to_all(produced, 'seq', split_axis=1, concat_axis=1, tiled=True)]
    all_gather x2 -> x0, waiting for transfers between devices: 140 us -> none  [the longest x1 93.5 us: local(): shard_rows = lax.all_gather(key_block, 'seq', axis=0, tiled=True)]
    reduce_scatter x1 -> x0, waiting for transfers between devices: 71.7 us -> none  [local(): lax.psum_scatter(jnp.dot(by_heads, proj_full, preferred_element_type=jnp....]
  transfers between devices with their start and end apart: 4 -> 0, of which waited for: 3 -> 0; matrix products, arithmetic and copies ran while one was open for 2% -> 0% of each run, Pallas kernels for 0% -> 0%
where the time goes in v1:
time: 2730 us; the launch traced here: 2720 us
  blocking collectives  2240 us (82%)
  Pallas kernels  480 us (18%)
    all_gather x2, blocking collectives, table(): lax.all_gather(a[0].T.reshape(1, 128), ('req', 'seq'), axis=0, tiled=True)  2240 us
    pallas_call x1, Pallas kernels, attention(): pl.pallas_call(attention_kernel, name='attention', out_shape=[jax.ShapeDt...  288 us
    pallas_call x1, Pallas kernels, experts(): pl.pallas_call(experts_kernel, name='experts', out_shape=jax.ShapeDtypeSt...  192 us

profile of v1, /device:TPU:6, one launch (start us, length us, event | category | flops | bytes accessed | tf_op | source)
XLA Modules:
  0.0 2722.7 jit_solution(10848962957135092310)
XLA Ops:
  0.0 0.0 copy-start
  0.0 0.0 copy-start.1
  0.0 0.8 reshape.26
  0.8 1021.3 %all-gather.1 = f32[512,1,128]{2,1,0:T(1,128)S(1)} all-gather(f32[1,1,128]{2,1,0:T(1,128)S(1)} %reshape.26), channel_id=1, replica_groups=mesh['req'=32,'seq'=16] {'req','seq'}, dimensions={0}, use_global_device_ids=true | all-gather | bytes 262656 | tf_op jit(solution)/shard_map/all_gather | solution.py:453
  1022.1 0.1 reshape_squeeze.7
  1022.2 0.2 copy.19
  1022.4 0.9 reshape.23.gt_ref
  1023.3 0.8 reshape.24
  1024.1 1214.8 %all-gather = s32[512,1,128]{2,1,0:T(1,128)S(1)} all-gather(s32[1,1,128]{2,1,0:T(1,128)S(1)} %reshape.24), channel_id=1, replica_groups=mesh['req'=32,'seq'=16] {'req','seq'}, dimensions={0}, use_global_device_ids=true | all-gather | bytes 262656 | tf_op jit(solution)/shard_map/all_gather | solution.py:453
  2238.9 0.1 reshape_squeeze.6
  2239.1 0.2 copy.17
  2239.3 0.9 reshape.20.rt_ref
  2240.2 0.0 copy-done
  2240.2 0.0 copy-done.1
  2240.2 0.7 pad_maximum_fusion.kv_ref
  2241.6 288.0 %attention.1 = (bf16[16,2048]{1,0:T(8,128)(2,1)}, bf16[16,2048]{1,0:T(8,128)(2,1)}) custom-call(s32[1]{0:T(128)S(6)} %copy.23.len_ref, bf16[128,1024]{1,0:T(8,128)(2,1)} %pad_maximum_fusion.kv_ref, bf16[16,4096]{1,0:T(8,128)(2,1)} %bitcast.39, bf16[64,256]{1,0:T(8,128)(2,1)} %bitcast.42, bf16[16,2048]{1,0:T(8,128)(2,1)} %bitcast.40, f32[1,2048]{1,0:T(1,128)} %bitcast.43), custom_call_target="tpu_custom_call" | custom-call | tf_op jit(solution)/shard_map/attention/pallas_call | solution.py:172
  2529.5 191.7 %experts.1 = bf16[16,2048]{1,0:T(8,128)(2,1)} custom-call(bf16[16,2048]{1,0:T(8,128)(2,1)} %get-tuple-element.7.normed_ref, bf16[16,2048]{1,0:T(8,128)(2,1)} %get-tuple-element.8.res_ref, s32[8,8,128]{2,1,0:T(8,128)} %reshape.20.rt_ref, f32[8,8,128]{2,1,0:T(8,128)} %reshape.23.gt_ref, bf16[2048,384]{1,0:T(8,128)(2,1)} %bitcast.31, bf16[192,2048]{1,0:T(8,128)(2,1)} %bitcast.34), custom_call_target="tpu_custom_call" | custom-call | tf_op jit(solution)/shard_map/experts/pallas_call | solution.py:420
  2721.3 1.5 copy.24
  (2 shorter events, 0.0 us)
Async XLA Ops:
  0.0 2240.2 %copy-start = (bf16[1,112,1024]{2,1,0:T(8,128)(2,1)S(1)}, bf16[1,112,1024]{2,1,0:T(8,128)(2,1)}, u32[]{:S(2)}) copy-start(bf16[1,112,1024]{2,1,0:T(8,128)(2,1)} %param.14) | copy-start | bytes 688132
  0.0 2240.2 %copy-start.1 = (bf16[1,16,1024]{2,1,0:T(8,128)(2,1)S(1)}, bf16[1,16,1024]{2,1,0:T(8,128)(2,1)}, u32[]{:S(2)}) copy-start(bf16[1,16,1024]{2,1,0:T(8,128)(2,1)} %param.13) | copy-start | bytes 98308

commit v2 on v1

--- a/solution.py
+++ b/solution.py
@@ -41,9 +41,9 @@
 
 
 def attention_kernel(
-    len_ref, kv_ref, q_ref, wt_ref, x_ref, gain_ref, res_ref, normed_ref,
-    kbuf, vbuf, qbuf, wbuf, att, pbuf, rbuf,
-    own_sem, kv_send, kv_recv, w_send, w_recv, sib_send, sib_recv, p_send, p_recv,
+    len_ref, kv_ref, q_ref, wt_ref, x_ref, gain_ref, mark_ref, res_ref, normed_ref, table_ref,
+    marks, near, far, kbuf, vbuf, qbuf, wbuf, att, pbuf, rbuf,
+    m_send, m_recv, n_send, n_recv, own_sem, kv_send, kv_recv, w_send, w_recv, sib_send, sib_recv, p_send, p_recv,
 ):
     req, seq = lax.axis_index("req"), lax.axis_index("seq")
     m, c = req // 2, req % 2
@@ -75,7 +75,20 @@
             wt_ref, wbuf.at[m, c], w_send.at[i], w_recv.at[i], (lax.rem(m + i, 16) * 2 + c, seq)
         )
 
+    def mark_copy(i):
+        dst_seq = lax.rem(seq + i, 16)
+        return remote(mark_ref, marks.at[seq], m_send.at[i], m_recv.at[i], (req, dst_seq))
+
+    def near_copy(i):
+        dst = (lax.rem(req + 8 * i, 32), seq)
+        return remote(near, far.at[i], n_send.at[i], n_recv.at[i], dst)
+
+    def mark_wait(i, _):
+        mark_copy(i).wait()
+        return 0
+
     def start(i, _):
+        mark_copy(i).start()
         for part in range(3):
             kv_copy(part, i).start()
         w_copy(i).start()
@@ -87,6 +100,7 @@
         src, dst = piece(part, seq, seq, 0)
         own.append(pltpu.make_async_copy(src, dst, own_sem.at[part]))
     own.append(pltpu.make_async_copy(wt_ref, wbuf.at[m, c], own_sem.at[3]))
+    own.append(pltpu.make_async_copy(mark_ref, marks.at[seq], own_sem.at[4]))
     for copy in own:
         copy.start()
     for copy in own:
@@ -101,6 +115,11 @@
         w_copy(i).wait()
         return 0
 
+    lax.fori_loop(1, 16, mark_wait, 0)
+    for n in range(8):
+        near[n] = marks[n] + marks[8 + n]
+    for i in range(1, 4):
+        near_copy(i).start()
     lax.fori_loop(1, 16, w_wait, 0)
     sib = remote(wbuf.at[:, c], wbuf.at[:, c], sib_send, sib_recv, sibling)
     sib.start()
@@ -154,6 +173,10 @@
         return 0
 
     lax.fori_loop(1, 16, p_start, 0)
+    for i in range(1, 4):
+        near_copy(i).wait()
+    for n in range(8):
+        table_ref[n] = near[n] + far[1, n] + far[2, n] + far[3, n]
     rbuf[0] = pbuf[pl.ds(pl.multiple_of(seq * 16, 16), 16), :]
     lax.fori_loop(1, 16, p_wait, 0)
     projected = lax.fori_loop(
@@ -166,16 +189,20 @@
     normed_ref[...] = (r * lax.rsqrt(mean + EPS) * gain_ref[...]).astype(BF)
 
 
-def attention(cached_len, kv, q, wt, x, gain):
+def attention(cached_len, kv, q, wt, x, gain, mark):
     vm = pl.BlockSpec(memory_space=pltpu.VMEM)
     dma = pltpu.SemaphoreType.DMA
     return pl.pallas_call(
         attention_kernel,
         name="attention",
-        out_shape=[jax.ShapeDtypeStruct((16, D), BF)] * 2,
-        in_specs=[pl.BlockSpec(memory_space=pltpu.SMEM)] + [vm] * 5,
-        out_specs=[vm] * 2,
+        out_shape=[jax.ShapeDtypeStruct((16, D), BF)] * 2
+        + [jax.ShapeDtypeStruct((8, 16, 128), F32)],
+        in_specs=[pl.BlockSpec(memory_space=pltpu.SMEM)] + [vm] * 6,
+        out_specs=[vm] * 3,
         scratch_shapes=[
+            pltpu.VMEM((16, 16, 128), F32),
+            pltpu.VMEM((8, 16, 128), F32),
+            pltpu.VMEM((4, 8, 16, 128), F32),
             pltpu.VMEM((2048, HD), BF),
             pltpu.VMEM((2048, HD), BF),
             pltpu.VMEM((256, 256), BF),
@@ -183,18 +210,20 @@
             pltpu.VMEM((256, 256), BF),
             pltpu.VMEM((256, D), BF),
             pltpu.VMEM((16, 16, D), BF),
-            dma((4,)),
+            dma((16,)), dma((16,)),
+            dma((4,)), dma((4,)),
+            dma((5,)),
             dma((3, 16)), dma((3, 16)),
             dma((16,)), dma((16,)),
             dma, dma,
             dma((16,)), dma((16,)),
         ],
         compiler_params=pltpu.CompilerParams(collective_id=0, has_side_effects=True),
-    )(cached_len, kv, q, wt, x, gain)
+    )(cached_len, kv, q, wt, x, gain, mark)
 
 
 def experts_kernel(
-    normed_ref, res_ref, rt_ref, gt_ref, wg_ref, wd_ref, out_ref,
+    normed_ref, res_ref, table_ref, wg_ref, wd_ref, out_ref,
     tok, comb, xs, xr, po, pr, sl, rl, sr, rr, fs, fr,
     z_send, z_recv, y_send, y_recv, x_send, x_recv, b_send, b_recv, r_send, r_recv, f_send, f_recv,
 ):
@@ -246,17 +275,17 @@
 
     def select(o):
         y0 = lax.rem(y + 8 - o, 8)
-        rt, gt = rt_ref[y0], gt_ref[y0]
+        table = table_ref[y0]
         row = lax.broadcasted_iota(jnp.int32, (128, 128), 0)
         col = lax.broadcasted_iota(jnp.int32, (128, 128), 1)
-        expert = 4 * (zhi * 8 + ((q + (row >> 4)) & 7)) + seq // 4
+        expert = (4 * (zhi * 8 + ((q + (row >> 4)) & 7)) + seq // 4).astype(F32)
         same = ((row >> 1) & 7) == (col >> 4)
         match = jnp.zeros((128, 128), F32)
         gate = jnp.zeros((128, 128), F32)
         for k in range(8):
-            hit = same & (rt[k : k + 1, :] == expert)
+            hit = same & (table[k : k + 1, :] == expert)
             match = jnp.where(hit, 1.0, match)
-            gate = jnp.where(hit, gt[k : k + 1, :], gate)
+            gate = jnp.where(hit, table[8 + k : 9 + k, :], gate)
         before = jnp.where(row < col, 1.0, 0.0).astype(BF)
         rank = jnp.dot(match.astype(BF), before, preferred_element_type=F32)
         pick = jnp.where(rank == (row & 1).astype(F32), match, 0.0)
@@ -412,7 +441,7 @@
     lax.fori_loop(0, 8, sent, 0)
 
 
-def experts(normed, residual, rt, gt, wg, wd):
+def experts(normed, residual, table, wg, wd):
     vm = pl.BlockSpec(memory_space=pltpu.VMEM)
     dma = pltpu.SemaphoreType.DMA
     big = pltpu.VMEM((8, 8, 16, D), BF)
@@ -421,7 +450,7 @@
         experts_kernel,
         name="experts",
         out_shape=jax.ShapeDtypeStruct((16, D), BF),
-        in_specs=[vm] * 6,
+        in_specs=[vm] * 5,
         out_specs=vm,
         scratch_shapes=[
             pltpu.VMEM((8, 128, D), BF),
@@ -440,27 +469,21 @@
         compiler_params=pltpu.CompilerParams(
             collective_id=1, has_side_effects=True, vmem_limit_bytes=56 * 1024 * 1024
         ),
-    )(normed, residual, rt, gt, wg, wd)
+    )(normed, residual, table, wg, wd)
 
 
 def local(
     layer_input, queries, fresh_kv, cache_kv, cached_len, out_weight, norm_gain,
     routes, route_gates, w_gate_up, w_down,
 ):
-    x, y, z, c = coords()
-
-    def table(a):
-        whole = lax.all_gather(a[0].T.reshape(1, 128), ("req", "seq"), axis=0, tiled=True)
-        whole = whole.reshape(4, 8, 2, 8, 128)
-        mine = lax.dynamic_slice_in_dim(whole, x * 2 + c, 1, axis=1)[:, 0]
-        return mine.reshape(4, 2, 8, 8, 16).transpose(2, 3, 0, 1, 4).reshape(8, 8, 128)
-
-    rt, gt = table(routes), table(route_gates)
+    z = coords()[2]
+    mark = jnp.concatenate([routes[0].T.astype(F32), route_gates[0].T], 0)
+    mark = jnp.where(jnp.arange(128)[None] // 16 == z, jnp.tile(mark, (1, 8)), 0.0)
     kv = jnp.concatenate([cache_kv[0], fresh_kv[0]], 0)
-    residual, normed = attention(
-        cached_len, kv, queries[0], out_weight.T, layer_input[0], norm_gain[None]
+    residual, normed, table = attention(
+        cached_len, kv, queries[0], out_weight.T, layer_input[0], norm_gain[None], mark
     )
-    return experts(normed, residual, rt, gt, w_gate_up[0], w_down[0])[None]
+    return experts(normed, residual, table, w_gate_up[0], w_down[0])[None]
 
 
 def solution(mesh):

time: 2730 us -> 268 us (0.10)
  blocking collectives: 2240 us -> 0 us
  Pallas kernels: 480 us -> 262 us
    all_gather x2 -> x0, blocking collectives: 2240 us -> none  [table(): lax.all_gather(a[0].T.reshape(1, 128), ('req', 'seq'), axis=0, tiled=True)]
    pallas_call x1, Pallas kernels: 288 us -> 79 us  [attention(): pl.pallas_call(attention_kernel, name='attention', out_shape=[jax.ShapeDt...]
where the time goes in v2:
time: 268 us
  Pallas kernels  262 us (98%)
  other arithmetic  3.66 us (1%)
    pallas_call x1, Pallas kernels, experts(): pl.pallas_call(experts_kernel, name='experts', out_shape=jax.ShapeDtypeSt...  183 us
    pallas_call x1, Pallas kernels, attention(): pl.pallas_call(attention_kernel, name='attention', out_shape=[jax.ShapeDt...  79 us

profile of v2, /device:TPU:6, one launch (start us, length us, event | category | flops | bytes accessed | tf_op | source)
XLA Modules:
  0.0 267.6 jit_solution(5490409569109794761)
XLA Ops:
  0.7 0.7 convert_bitcast_fusion
  1.4 0.7 pad_maximum_fusion.1
  2.1 0.1 tile.10
  2.1 0.6 broadcast_select_fusion.mark_ref
  2.7 1.7 pad_maximum_fusion.kv_ref
  4.4 79.0 %attention.1 = (bf16[16,2048]{1,0:T(8,128)(2,1)}, bf16[16,2048]{1,0:T(8,128)(2,1)}, f32[8,16,128]{2,1,0:T(8,128)}) custom-call(s32[1]{0:T(128)S(6)} %copy.13.len_ref, bf16[128,1024]{1,0:T(8,128)(2,1)} %pad_maximum_fusion.kv_ref, bf16[16,4096]{1,0:T(8,128)(2,1)} %bitcast.20, bf16[64,256]{1,0:T(8,128)(2,1)} %bitcast.23, bf16[16,2048]{1,0:T(8,128)(2,1)} %bitcast.21, ...), custom_call_target="tpu_custom_call" | custom-call | tf_op jit(solution)/shard_map/attention/pallas_call | solution.py:195
  83.5 182.7 %experts.1 = bf16[16,2048]{1,0:T(8,128)(2,1)} custom-call(bf16[16,2048]{1,0:T(8,128)(2,1)} %get-tuple-element.8.normed_ref, bf16[16,2048]{1,0:T(8,128)(2,1)} %get-tuple-element.9.res_ref, f32[8,16,128]{2,1,0:T(8,128)} %get-tuple-element.10.table_ref, bf16[2048,384]{1,0:T(8,128)(2,1)} %bitcast.16, bf16[192,2048]{1,0:T(8,128)(2,1)} %bitcast.17), custom_call_target="tpu_custom_call" | custom-call | tf_op jit(solution)/shard_map/experts/pallas_call | solution.py:449
  266.2 1.5 copy.14
  (2 shorter events, 0.0 us)

commit v3 on v2

--- a/solution.py
+++ b/solution.py
@@ -222,60 +222,94 @@
     )(cached_len, kv, q, wt, x, gain, mark)
 
 
+ORDER = (0, 1, 7, 2, 6, 3, 5, 4)
+PLACE = {o: i for i, o in enumerate(ORDER)}
+CHUNKS = ((0, 1), (7, 2), (6, 3), (5, 4))
+
+
 def experts_kernel(
     normed_ref, res_ref, table_ref, wg_ref, wd_ref, out_ref,
-    tok, comb, xs, xr, po, pr, sl, rl, sr, rr, fs, fr,
+    tok, comb, xs, xr, po, pr, part, sl, rl, sr, rr, fs, fr,
     z_send, z_recv, y_send, y_recv, x_send, x_recv, b_send, b_recv, r_send, r_recv, f_send, f_recv,
 ):
     x, y, z, c = coords()
     q = x * 2 + c
+    seq, zhi = (z % 2) * 8 + y, z // 2
     right, left = device(x, lax.rem(y + 1, 8), z, c), device(x, lax.rem(y + 7, 8), z, c)
 
     def at_q(j):
         n = lax.rem(q + j, 8)
         return device(n // 2, y, z, lax.rem(n, 2))
 
-    zs = [device(x, y, lax.rem(z + i, 8), c) for i in range(1, 8)]
-    greet(zs + [right, left] + [at_q(j) for j in range(1, 8)])
-
-    own_rows = pl.ds(pl.multiple_of(z * 16, 16), 16)
-
-    def z_copy(i):
-        dev = device(x, y, lax.rem(z + i, 8), c)
-        return remote(normed_ref, tok.at[0, own_rows], z_send.at[i], z_recv.at[i], dev)
-
-    for i in range(1, 8):
-        z_copy(i).start()
-    tok[0, own_rows] = normed_ref[...]
-    for i in range(1, 8):
-        z_copy(i).wait()
+    def at_z(i):
+        return device(x, y, lax.rem(z + i, 8), c)
+
+    greet([at_z(i) for i in range(1, 8)] + [right, left] + [at_q(j) for j in range(1, 8)])
+
+    where_z = {r: (ch, zz) for ch, rs in enumerate(CHUNKS) for zz, r in enumerate(rs)}
+
+    def z_copy(r):
+        ch, zz = where_z[r]
+        return remote(
+            normed_ref, tok.at[ch, 0, zz * 16 : zz * 16 + 16], z_send.at[r], z_recv.at[r], at_z(r)
+        )
 
     def half(h):
         return pl.ds(h * 1024, 1024)
 
-    def y_copy(way, t, h):
-        if way == 0:
-            a, b, dev = t, t + 1, right
-        else:
-            a, b, dev = (8 - t) % 8, 7 - t, left
+    def whole():
+        return pl.ds(0, D)
+
+    def y_copy(way, t, ch):
+        a, b, dev = (t, t + 1, right) if way == 0 else ((8 - t) % 8, 7 - t, left)
+        cols = whole() if t < 3 else half(way)
         return remote(
-            tok.at[a, :, half(h)], tok.at[b, :, half(h)], y_send.at[way, t, h], y_recv.at[way, t, h], dev
+            tok.at[ch, PLACE[a], :, cols], tok.at[ch, PLACE[b], :, cols],
+            y_send.at[way, t, ch], y_recv.at[way, t, ch], dev,
         )
 
-    def steps(t):
-        return [(0, 0), (1, 0), (0, 1), (1, 1)] if t < 3 else [(0, 0), (1, 1)]
-
-    def x_copy(o, j):
-        return remote(xs.at[o, j], xr.at[o, j], x_send.at[o, j], x_recv.at[o, j], at_q(j))
-
-    def b_copy(o, j):
-        return remote(po.at[o, j], pr.at[o, j], b_send.at[o, j], b_recv.at[o, j], at_q(8 - j))
-
-    seq, zhi = (z % 2) * 8 + y, z // 2
-
-    def select(o):
-        y0 = lax.rem(y + 8 - o, 8)
-        table = table_ref[y0]
+    def r_copy(way, t, ch):
+        src, dst, dev = (sl, rl, left) if way == 0 else (sr, rr, right)
+        cols = whole() if t > 0 else half(way)
+        return remote(
+            src.at[ch, t, :, cols], dst.at[ch, t, :, cols],
+            r_send.at[way, t, ch], r_recv.at[way, t, ch], dev,
+        )
+
+    def x_copy(u, j):
+        return remote(xs.at[u, j], xr.at[u, j], x_send.at[u, j], x_recv.at[u, j], at_q(j))
+
+    def b_copy(u, j):
+        return remote(po.at[u, j], pr.at[u, j], b_send.at[u, j], b_recv.at[u, j], at_q(8 - j))
+
+    def f_copy(r):
+        ch, zz = where_z[r]
+        return remote(
+            fs.at[ch, zz * 16 : zz * 16 + 16], fr.at[r], f_send.at[r], f_recv.at[r], at_z(8 - r)
+        )
+
+    def gather(ch, t):
+        if t == 0:
+            for r in CHUNKS[ch]:
+                if r:
+                    z_copy(r).wait_recv()
+        for way in range(2):
+            if t > 0:
+                y_copy(way, t - 1, ch).wait_recv()
+            if t < 4:
+                y_copy(way, t, ch).start()
+
+    def select(ch, g):
+        u = 2 * ch + g
+        lane = lax.broadcasted_iota(jnp.int32, (16, 128), 1)
+        table = jnp.zeros((16, 128), F32)
+        for p in range(4):
+            y0 = lax.rem(y + 8 - ORDER[4 * g + p], 8)
+            for zz in range(2):
+                z0 = lax.rem(z + 8 - CHUNKS[ch][zz], 8)
+                n = 2 * p + zz
+                rolled = pltpu.roll(table_ref[y0], lax.rem(n * 16 + 128 - z0 * 16, 128), 1)
+                table = jnp.where((lane >> 4) == n, rolled, table)
         row = lax.broadcasted_iota(jnp.int32, (128, 128), 0)
         col = lax.broadcasted_iota(jnp.int32, (128, 128), 1)
         expert = (4 * (zhi * 8 + ((q + (row >> 4)) & 7)) + seq // 4).astype(F32)
@@ -289,151 +323,161 @@
         before = jnp.where(row < col, 1.0, 0.0).astype(BF)
         rank = jnp.dot(match.astype(BF), before, preferred_element_type=F32)
         pick = jnp.where(rank == (row & 1).astype(F32), match, 0.0)
-        comb[o] = (pick * gate).T.astype(BF)
+        comb[u] = (pick * gate).T.astype(BF)
         pick = pick.astype(BF)
 
         def tile(n, _):
             cols = pl.ds(pl.multiple_of(n * 512, 512), 512)
-            rows = jnp.dot(pick, tok[o, :, cols], preferred_element_type=F32).astype(BF)
-            xs[o, :, :, cols] = rows.reshape(8, 16, 512)
-            xr[o, 0, :, cols] = rows[:16]
+            rows = tok[ch, 4 * g : 4 * g + 4, :, cols].reshape(128, 512)
+            rows = jnp.dot(pick, rows, preferred_element_type=F32).astype(BF)
+            xs[u, :, :, cols] = rows.reshape(8, 16, 512)
+            xr[u, 0, :, cols] = rows[:16]
             return 0
 
         lax.fori_loop(0, 4, tile, 0)
 
         def send(j, _):
-            x_copy(o, j).start()
+            x_copy(u, j).start()
             return 0
 
         lax.fori_loop(1, 8, send, 0)
 
-    def feed(o):
+    def feed(ch, g):
+        u = 2 * ch + g
+
         def arrive(j, _):
-            x_copy(o, j).wait_recv()
+            x_copy(u, j).wait_recv()
             return 0
 
         lax.fori_loop(1, 8, arrive, 0)
-        both = jnp.dot(xr[o].reshape(128, D), wg_ref[...], preferred_element_type=F32)
-        g, u = both[:, :192], both[:, 192:]
-        hidden = (g / (1.0 + jnp.exp(-g)) * u).astype(BF)
+        both = jnp.dot(xr[u].reshape(128, D), wg_ref[...], preferred_element_type=F32)
+        v, w = both[:, :192], both[:, 192:]
+        hidden = (v / (1.0 + jnp.exp(-v)) * w).astype(BF)
 
         def tile(n, _):
             cols = pl.ds(pl.multiple_of(n * 512, 512), 512)
             rows = jnp.dot(hidden, wd_ref[:, cols], preferred_element_type=F32).astype(BF)
-            po[o, :, :, cols] = rows.reshape(8, 16, 512)
-            pr[o, 0, :, cols] = rows[:16]
+            po[u, :, :, cols] = rows.reshape(8, 16, 512)
+            pr[u, 0, :, cols] = rows[:16]
             return 0
 
         lax.fori_loop(0, 4, tile, 0)
 
         def send(j, _):
-            b_copy(o, j).start()
+            b_copy(u, j).start()
             return 0
 
         lax.fori_loop(1, 8, send, 0)
 
-    def returned(o):
+    def combine(ch, g):
+        u = 2 * ch + g
+
         def arrive(j, _):
-            b_copy(o, j).wait_recv()
+            b_copy(u, j).wait_recv()
             return 0
 
         lax.fori_loop(1, 8, arrive, 0)
 
-    def combined(o, cols):
-        rows = pr[o, :, :, cols].reshape(128, cols.size)
-        return jnp.dot(comb[o], rows, preferred_element_type=F32)
-
-    def pair(f, o):
-        def one(i, _):
-            f(jnp.where(i == 0, o, 8 - o))
-            return 0
-
-        lax.fori_loop(0, 2, one, 0)
-
-    for way, h in steps(0):
-        y_copy(way, 0, h).start()
-    select(0)
-    for t in range(1, 4):
-        for way, h in steps(t - 1):
-            y_copy(way, t - 1, h).wait_recv()
-            if (way, h) in steps(t):
-                y_copy(way, t, h).start()
-        pair(select, t)
-        if t == 1:
-            feed(0)
-        else:
-            pair(feed, t - 1)
-    for way, h in steps(3):
-        y_copy(way, 3, h).wait_recv()
-    select(4)
-    pair(feed, 3)
-    feed(4)
-
-    def r_copy(way, t, h):
-        src, dst, dev = (sl, rl, left) if way == 0 else (sr, rr, right)
-        return remote(
-            src.at[t, :, half(h)], dst.at[t, :, half(h)], r_send.at[way, t, h], r_recv.at[way, t, h], dev
-        )
-
-    def r_steps(t):
-        return [(0, 0), (1, 1)] if t == 0 else [(0, 0), (1, 1), (0, 1), (1, 0)]
-
-    for t in range(4):
-        for o in {4 - t, 4 + t}:
-            returned(o)
-        for way, h in r_steps(t):
+        def tile(n, _):
+            cols = pl.ds(pl.multiple_of(n * 512, 512), 512)
+            rows = pr[u, :, :, cols].reshape(128, 512)
+            rows = jnp.dot(comb[u], rows, preferred_element_type=F32)
+            part[ch, 4 * g : 4 * g + 4, :, cols] = rows.reshape(4, 32, 512)
+            return 0
+
+        lax.fori_loop(0, 4, tile, 0)
+
+    def scatter(ch, t):
+        for way in range(2):
             o = 4 - t if way == 0 else 4 + t
-            came = t > 0 and (way, h) in r_steps(t - 1)
-            if came:
-                r_copy(way, t - 1, h).wait_recv()
             src, dst = (sl, rl) if way == 0 else (sr, rr)
-
-            def tile(n, _):
-                cols = pl.ds(pl.multiple_of(h * 1024 + n * 512, 512), 512)
-                part = combined(o, cols)
-                if came:
-                    part = part + dst[t - 1, :, cols].astype(F32)
-                src[t, :, cols] = part.astype(BF)
-                return 0
-
-            lax.fori_loop(0, 2, tile, 0)
-            r_copy(way, t, h).start()
-
-    returned(0)
-    for way, h in r_steps(3):
-        r_copy(way, 3, h).wait_recv()
-
-    def total(n, _):
-        cols = pl.ds(pl.multiple_of(n * 512, 512), 512)
-        part = combined(0, cols) + rl[3, :, cols].astype(F32) + rr[3, :, cols].astype(F32)
-        fs[:, cols] = part.astype(BF)
-        return 0
-
-    lax.fori_loop(0, 4, total, 0)
-
-    def f_copy(i):
-        n = lax.rem(z + i, 8)
-        rows = pl.ds(pl.multiple_of(n * 16, 16), 16)
-        return remote(fs.at[rows, :], fr.at[i], f_send.at[i], f_recv.at[i], device(x, y, n, c))
-
-    for i in range(1, 8):
-        f_copy(i).start()
-    acc = res_ref[...].astype(F32) + fs[own_rows, :].astype(F32)
-    for i in range(1, 8):
-        f_copy(i).wait()
-        acc = acc + fr[i].astype(F32)
+            if t > 0:
+                r_copy(way, t - 1, ch).wait_recv()
+            for h in range(2):
+                if t == 0 and h != way:
+                    continue
+                value = part[ch, PLACE[o], :, half(h)]
+                if t > 1 or (t == 1 and h == way):
+                    value = value + dst[ch, t - 1, :, half(h)].astype(F32)
+                src[ch, t, :, half(h)] = value.astype(BF)
+            r_copy(way, t, ch).start()
+
+    def finish(ch):
+        for way in range(2):
+            r_copy(way, 3, ch).wait_recv()
+        for h in range(2):
+            value = part[ch, 0, :, half(h)] + rl[ch, 3, :, half(h)].astype(F32)
+            fs[ch, :, half(h)] = (value + rr[ch, 3, :, half(h)].astype(F32)).astype(BF)
+        for r in CHUNKS[ch]:
+            if r:
+                f_copy(r).start()
+
+    for r in (1, 7, 2, 6, 3, 5, 4):
+        z_copy(r).start()
+    tok[0, 0, :16] = normed_ref[...]
+
+    gather(0, 0)
+    gather(0, 1)
+    gather(1, 0)
+    gather(0, 2)
+    select(0, 0)
+    gather(1, 1)
+    gather(0, 3)
+    gather(1, 2)
+    gather(0, 4)
+    select(0, 1)
+    gather(1, 3)
+    gather(1, 4)
+    for ch in range(5):
+        if ch + 2 < 4:
+            gather(ch + 2, 0)
+        if ch + 1 < 4:
+            select(ch + 1, 0)
+        if ch < 4:
+            feed(ch, 0)
+        if ch + 2 < 4:
+            gather(ch + 2, 1)
+        if ch + 1 < 4:
+            select(ch + 1, 1)
+        if ch > 0:
+            combine(ch - 1, 1)
+            scatter(ch - 1, 0)
+        if ch < 4:
+            feed(ch, 1)
+        if ch + 2 < 4:
+            gather(ch + 2, 2)
+        if ch > 0:
+            combine(ch - 1, 0)
+            scatter(ch - 1, 1)
+        if ch + 2 < 4:
+            gather(ch + 2, 3)
+        if ch > 0:
+            scatter(ch - 1, 2)
+        if ch + 2 < 4:
+            gather(ch + 2, 4)
+        if ch > 0:
+            scatter(ch - 1, 3)
+            finish(ch - 1)
+
+    acc = res_ref[...].astype(F32) + fs[0, :16].astype(F32)
+    for r in (1, 7, 2, 6, 3, 5, 4):
+        f_copy(r).wait_recv()
+        acc = acc + fr[r].astype(F32)
     out_ref[...] = acc.astype(BF)
 
-    for t in range(4):
-        for way, h in steps(t):
-            y_copy(way, t, h).wait_send()
-        for way, h in r_steps(t):
-            r_copy(way, t, h).wait_send()
-
-    def sent(o, _):
+    for r in range(1, 8):
+        z_copy(r).wait_send()
+        f_copy(r).wait_send()
+    for ch in range(4):
+        for t in range(4):
+            for way in range(2):
+                y_copy(way, t, ch).wait_send()
+                r_copy(way, t, ch).wait_send()
+
+    def sent(u, _):
         def one(j, _):
-            x_copy(o, j).wait_send()
-            b_copy(o, j).wait_send()
+            x_copy(u, j).wait_send()
+            b_copy(u, j).wait_send()
             return 0
 
         return lax.fori_loop(1, 8, one, 0)
@@ -445,7 +489,7 @@
     vm = pl.BlockSpec(memory_space=pltpu.VMEM)
     dma = pltpu.SemaphoreType.DMA
     big = pltpu.VMEM((8, 8, 16, D), BF)
-    hop = pltpu.VMEM((4, 128, D), BF)
+    hop = pltpu.VMEM((4, 4, 32, D), BF)
     return pl.pallas_call(
         experts_kernel,
         name="experts",
@@ -453,17 +497,18 @@
         in_specs=[vm] * 5,
         out_specs=vm,
         scratch_shapes=[
-            pltpu.VMEM((8, 128, D), BF),
+            pltpu.VMEM((4, 8, 32, D), BF),
             pltpu.VMEM((8, 128, 128), BF),
             big, big, big, big,
+            pltpu.VMEM((4, 8, 32, D), F32),
             hop, hop, hop, hop,
-            pltpu.VMEM((128, D), BF),
+            pltpu.VMEM((4, 32, D), BF),
             pltpu.VMEM((8, 16, D), BF),
             dma((8,)), dma((8,)),
-            dma((2, 4, 2)), dma((2, 4, 2)),
+            dma((2, 4, 4)), dma((2, 4, 4)),
             dma((8, 8)), dma((8, 8)),
             dma((8, 8)), dma((8, 8)),
-            dma((2, 4, 2)), dma((2, 4, 2)),
+            dma((2, 4, 4)), dma((2, 4, 4)),
             dma((8,)), dma((8,)),
         ],
         compiler_params=pltpu.CompilerParams(

time: 268 us -> 247 us (0.922)
  Pallas kernels: 262 us -> 239 us
    pallas_call x1, Pallas kernels: 183 us -> 160 us  [experts(): pl.pallas_call(experts_kernel, name='experts', out_shape=jax.ShapeDtypeSt...]
where the time goes in v3:
time: 247 us; the launch traced here: 245 us
  Pallas kernels  239 us (97%)
  other arithmetic  3.66 us (1%)
    pallas_call x1, Pallas kernels, experts(): pl.pallas_call(experts_kernel, name='experts', out_shape=jax.ShapeDtypeSt...  160 us
    pallas_call x1, Pallas kernels, attention(): pl.pallas_call(attention_kernel, name='attention', out_shape=[jax.ShapeDt...  79 us

profile of v3, /device:TPU:6, one launch (start us, length us, event | category | flops | bytes accessed | tf_op | source)
XLA Modules:
  0.0 244.6 jit_solution(12031697058401443968)
XLA Ops:
  0.7 0.7 convert_bitcast_fusion
  1.4 0.7 pad_maximum_fusion.1
  2.1 0.1 tile.10
  2.1 0.6 broadcast_select_fusion.mark_ref
  2.7 1.7 pad_maximum_fusion.kv_ref
  4.4 79.0 %attention.1 = (bf16[16,2048]{1,0:T(8,128)(2,1)}, bf16[16,2048]{1,0:T(8,128)(2,1)}, f32[8,16,128]{2,1,0:T(8,128)}) custom-call(s32[1]{0:T(128)S(6)} %copy.13.len_ref, bf16[128,1024]{1,0:T(8,128)(2,1)} %pad_maximum_fusion.kv_ref, bf16[16,4096]{1,0:T(8,128)(2,1)} %bitcast.20, bf16[64,256]{1,0:T(8,128)(2,1)} %bitcast.23, bf16[16,2048]{1,0:T(8,128)(2,1)} %bitcast.21, ...), custom_call_target="tpu_custom_call" | custom-call | tf_op jit(solution)/shard_map/attention/pallas_call | solution.py:195
  83.5 159.7 %experts.1 = bf16[16,2048]{1,0:T(8,128)(2,1)} custom-call(bf16[16,2048]{1,0:T(8,128)(2,1)} %get-tuple-element.8.normed_ref, bf16[16,2048]{1,0:T(8,128)(2,1)} %get-tuple-element.9.res_ref, f32[8,16,128]{2,1,0:T(8,128)} %get-tuple-element.10.table_ref, bf16[2048,384]{1,0:T(8,128)(2,1)} %bitcast.16, bf16[192,2048]{1,0:T(8,128)(2,1)} %bitcast.17), custom_call_target="tpu_custom_call" | custom-call | tf_op jit(solution)/shard_map/experts/pallas_call | solution.py:493
  243.1 1.5 copy.14
  (2 shorter events, 0.0 us)

commit v4 on v3

--- a/solution.py
+++ b/solution.py
@@ -127,14 +127,21 @@
 
     length = len_ref[0]
     scale = 1.0 / math.sqrt(HD)
-    for head in range(2):
-
-        def tile(i, _):
-            rows = pl.ds(pl.multiple_of(i * 64, 64), 64)
+    sib.wait()
+
+    def p_copy(dst_seq):
+        i = lax.rem(dst_seq + 16 - seq, 16)
+        rows = pl.ds(pl.multiple_of(dst_seq * 16, 16), 16)
+        return remote(pbuf.at[rows, :], rbuf.at[i], p_send.at[i], p_recv.at[i], (req, dst_seq))
+
+    def tile(step, _):
+        quad = lax.rem(seq // 4 + 1 + step, 4)
+        rows = pl.ds(pl.multiple_of(quad * 64, 64), 64)
+        for head in range(2):
             q = qbuf[rows, head * HD : (head + 1) * HD]
             s = lax.dot_general(q, kbuf[...], NT, preferred_element_type=F32) * scale
             col = lax.broadcasted_iota(jnp.int32, (64, D), 1)
-            tok = lax.broadcasted_iota(jnp.int32, (64, D), 0) + i * 64
+            tok = lax.broadcasted_iota(jnp.int32, (64, D), 0) + quad * 64
             src, within = col >> 7, col & 127
             behind = jnp.where(
                 within < 112, src * 112 + within - length, src * 16 + within - 113 - tok
@@ -145,34 +152,33 @@
             total = jnp.sum(w, axis=-1, keepdims=True)
             mixed = jnp.dot(w.astype(BF), vbuf[...], preferred_element_type=F32)
             att[rows, head * HD : (head + 1) * HD] = (mixed / total).astype(BF)
-            return 0
-
-        lax.fori_loop(0, 4, tile, 0)
-
-    sib.wait()
-
-    def project(i, _):
-        w = wbuf[pl.ds(i * 4, 4)].reshape(512, 256)
-        cols = pl.ds(pl.multiple_of(i * 512, 512), 512)
-        pbuf[:, cols] = lax.dot_general(att[...], w, NT, preferred_element_type=F32).astype(BF)
+
+        def project(i, _):
+            w = wbuf[pl.ds(i * 4, 4)].reshape(512, 256)
+            cols = pl.ds(pl.multiple_of(i * 512, 512), 512)
+            out = lax.dot_general(att[rows, :], w, NT, preferred_element_type=F32)
+            pbuf[rows, cols] = out.astype(BF)
+            return 0
+
+        lax.fori_loop(0, 4, project, 0)
+
+        def send(n, _):
+            dst_seq = quad * 4 + lax.rem(seq + n, 4)
+
+            @pl.when(dst_seq != seq)
+            def _():
+                p_copy(dst_seq).start()
+
+            return 0
+
+        return lax.fori_loop(0, 4, send, 0)
+
+    lax.fori_loop(0, 4, tile, 0)
+
+    def p_wait(i, _):
+        p_copy(lax.rem(seq + i, 16)).wait()
         return 0
 
-    lax.fori_loop(0, 4, project, 0)
-
-    def p_copy(i):
-        dst_seq = lax.rem(seq + i, 16)
-        rows = pl.ds(pl.multiple_of(dst_seq * 16, 16), 16)
-        return remote(pbuf.at[rows, :], rbuf.at[i], p_send.at[i], p_recv.at[i], (req, dst_seq))
-
-    def p_start(i, _):
-        p_copy(i).start()
-        return 0
-
-    def p_wait(i, _):
-        p_copy(i).wait()
-        return 0
-
-    lax.fori_loop(1, 16, p_start, 0)
     for i in range(1, 4):
         near_copy(i).wait()
     for n in range(8):
@@ -226,6 +232,73 @@
 PLACE = {o: i for i, o in enumerate(ORDER)}
 CHUNKS = ((0, 1), (7, 2), (6, 3), (5, 4))
 
+PLAN = (
+    ("g", 0, 0),
+    ("g", 1, 0),
+    ("g", 0, 1),
+    ("g", 1, 1),
+    ("g", 0, 2),
+    ("s", 0, 0),
+    ("g", 1, 2),
+    ("g", 2, 0),
+    ("s", 1, 0),
+    ("g", 1, 3),
+    ("g", 0, 3),
+    ("g", 3, 0),
+    ("f", 0, 0),
+    ("g", 1, 4),
+    ("g", 0, 4),
+    ("g", 2, 1),
+    ("s", 0, 1),
+    ("g", 3, 1),
+    ("g", 2, 2),
+    ("s", 1, 1),
+    ("g", 2, 3),
+    ("f", 0, 1),
+    ("f", 1, 1),
+    ("g", 2, 4),
+    ("c", 0, 1),
+    ("g", 3, 2),
+    ("s", 2, 1),
+    ("g", 3, 3),
+    ("f", 1, 0),
+    ("c", 1, 1),
+    ("s", 2, 0),
+    ("r", 0, 0),
+    ("g", 3, 4),
+    ("r", 1, 0),
+    ("s", 3, 1),
+    ("c", 1, 0),
+    ("r", 0, 1),
+    ("c", 0, 0),
+    ("r", 1, 1),
+    ("s", 3, 0),
+    ("f", 3, 1),
+    ("r", 0, 2),
+    ("r", 1, 2),
+    ("f", 2, 1),
+    ("f", 3, 0),
+    ("r", 1, 3),
+    ("f", 2, 0),
+    ("c", 3, 1),
+    ("r", 3, 0),
+    ("r", 0, 3),
+    ("c", 2, 1),
+    ("r", 2, 0),
+    ("r", 3, 1),
+    ("n", 1, 0),
+    ("r", 2, 1),
+    ("c", 3, 0),
+    ("r", 3, 2),
+    ("c", 2, 0),
+    ("r", 2, 2),
+    ("r", 3, 3),
+    ("r", 2, 3),
+    ("n", 0, 0),
+    ("n", 3, 0),
+    ("n", 2, 0),
+)
+
 
 def experts_kernel(
     normed_ref, res_ref, table_ref, wg_ref, wd_ref, out_ref,
@@ -233,18 +306,17 @@
     z_send, z_recv, y_send, y_recv, x_send, x_recv, b_send, b_recv, r_send, r_recv, f_send, f_recv,
 ):
     x, y, z, c = coords()
-    q = x * 2 + c
     seq, zhi = (z % 2) * 8 + y, z // 2
     right, left = device(x, lax.rem(y + 1, 8), z, c), device(x, lax.rem(y + 7, 8), z, c)
 
-    def at_q(j):
-        n = lax.rem(q + j, 8)
-        return device(n // 2, y, z, lax.rem(n, 2))
+    def at_x(j, back=False):
+        far = 4 - j // 2 if back else j // 2
+        return device(lax.rem(x + far, 4), y, z, lax.rem(c + j, 2))
 
     def at_z(i):
         return device(x, y, lax.rem(z + i, 8), c)
 
-    greet([at_z(i) for i in range(1, 8)] + [right, left] + [at_q(j) for j in range(1, 8)])
+    greet([at_z(i) for i in range(1, 8)] + [right, left] + [at_x(j) for j in range(1, 8)])
 
     where_z = {r: (ch, zz) for ch, rs in enumerate(CHUNKS) for zz, r in enumerate(rs)}
 
@@ -277,10 +349,10 @@
         )
 
     def x_copy(u, j):
-        return remote(xs.at[u, j], xr.at[u, j], x_send.at[u, j], x_recv.at[u, j], at_q(j))
+        return remote(xs.at[u, j], xr.at[u, j], x_send.at[u, j], x_recv.at[u, j], at_x(j))
 
     def b_copy(u, j):
-        return remote(po.at[u, j], pr.at[u, j], b_send.at[u, j], b_recv.at[u, j], at_q(8 - j))
+        return remote(po.at[u, j], pr.at[u, j], b_send.at[u, j], b_recv.at[u, j], at_x(j, True))
 
     def f_copy(r):
         ch, zz = where_z[r]
@@ -312,7 +384,8 @@
                 table = jnp.where((lane >> 4) == n, rolled, table)
         row = lax.broadcasted_iota(jnp.int32, (128, 128), 0)
         col = lax.broadcasted_iota(jnp.int32, (128, 128), 1)
-        expert = (4 * (zhi * 8 + ((q + (row >> 4)) & 7)) + seq // 4).astype(F32)
+        req = zhi * 8 + ((x + (row >> 5)) & 3) * 2 + ((c + (row >> 4)) & 1)
+        expert = (4 * req + seq // 4).astype(F32)
         same = ((row >> 1) & 7) == (col >> 4)
         match = jnp.zeros((128, 128), F32)
         gate = jnp.zeros((128, 128), F32)
@@ -416,48 +489,9 @@
         z_copy(r).start()
     tok[0, 0, :16] = normed_ref[...]
 
-    gather(0, 0)
-    gather(0, 1)
-    gather(1, 0)
-    gather(0, 2)
-    select(0, 0)
-    gather(1, 1)
-    gather(0, 3)
-    gather(1, 2)
-    gather(0, 4)
-    select(0, 1)
-    gather(1, 3)
-    gather(1, 4)
-    for ch in range(5):
-        if ch + 2 < 4:
-            gather(ch + 2, 0)
-        if ch + 1 < 4:
-            select(ch + 1, 0)
-        if ch < 4:
-            feed(ch, 0)
-        if ch + 2 < 4:
-            gather(ch + 2, 1)
-        if ch + 1 < 4:
-            select(ch + 1, 1)
-        if ch > 0:
-            combine(ch - 1, 1)
-            scatter(ch - 1, 0)
-        if ch < 4:
-            feed(ch, 1)
-        if ch + 2 < 4:
-            gather(ch + 2, 2)
-        if ch > 0:
-            combine(ch - 1, 0)
-            scatter(ch - 1, 1)
-        if ch + 2 < 4:
-            gather(ch + 2, 3)
-        if ch > 0:
-            scatter(ch - 1, 2)
-        if ch + 2 < 4:
-            gather(ch + 2, 4)
-        if ch > 0:
-            scatter(ch - 1, 3)
-            finish(ch - 1)
+    work = {"g": gather, "s": select, "f": feed, "c": combine, "r": scatter, "n": lambda ch, _: finish(ch)}
+    for kind, ch, i in PLAN:
+        work[kind](ch, i)
 
     acc = res_ref[...].astype(F32) + fs[0, :16].astype(F32)
     for r in (1, 7, 2, 6, 3, 5, 4):

time: 247 us -> 225 us (0.911)
  Pallas kernels: 239 us -> 217 us
    pallas_call x1, Pallas kernels: 160 us -> 141 us  [experts(): pl.pallas_call(experts_kernel, name='experts', out_shape=jax.ShapeDtypeSt...]
    pallas_call x1, Pallas kernels: 79 us -> 76.1 us  [attention(): pl.pallas_call(attention_kernel, name='attention', out_shape=[jax.ShapeDt...]
where the time goes in v4:
time: 225 us; the launch traced here: 223 us
  Pallas kernels  217 us (96%)
  other arithmetic  3.66 us (2%)
    pallas_call x1, Pallas kernels, experts(): pl.pallas_call(experts_kernel, name='experts', out_shape=jax.ShapeDtypeSt...  141 us
    pallas_call x1, Pallas kernels, attention(): pl.pallas_call(attention_kernel, name='attention', out_shape=[jax.ShapeDt...  76.1 us

profile of v4, /device:TPU:6, one launch (start us, length us, event | category | flops | bytes accessed | tf_op | source)
XLA Modules:
  0.0 223.3 jit_solution(10858532675480029945)
XLA Ops:
  0.7 0.7 convert_bitcast_fusion
  1.4 0.7 pad_maximum_fusion.1
  2.1 0.1 tile.10
  2.1 0.6 broadcast_select_fusion.mark_ref
  2.7 1.7 pad_maximum_fusion.kv_ref
  4.4 76.1 %attention.1 = (bf16[16,2048]{1,0:T(8,128)(2,1)}, bf16[16,2048]{1,0:T(8,128)(2,1)}, f32[8,16,128]{2,1,0:T(8,128)}) custom-call(s32[1]{0:T(128)S(6)} %copy.13.len_ref, bf16[128,1024]{1,0:T(8,128)(2,1)} %pad_maximum_fusion.kv_ref, bf16[16,4096]{1,0:T(8,128)(2,1)} %bitcast.20, bf16[64,256]{1,0:T(8,128)(2,1)} %bitcast.23, bf16[16,2048]{1,0:T(8,128)(2,1)} %bitcast.21, ...), custom_call_target="tpu_custom_call" | custom-call | tf_op jit(solution)/shard_map/attention/pallas_call | solution.py:201
  80.6 141.2 %experts.1 = bf16[16,2048]{1,0:T(8,128)(2,1)} custom-call(bf16[16,2048]{1,0:T(8,128)(2,1)} %get-tuple-element.8.normed_ref, bf16[16,2048]{1,0:T(8,128)(2,1)} %get-tuple-element.9.res_ref, f32[8,16,128]{2,1,0:T(8,128)} %get-tuple-element.10.table_ref, bf16[2048,384]{1,0:T(8,128)(2,1)} %bitcast.16, bf16[192,2048]{1,0:T(8,128)(2,1)} %bitcast.17), custom_call_target="tpu_custom_call" | custom-call | tf_op jit(solution)/shard_map/experts/pallas_call | solution.py:527
  221.8 1.5 copy.14
  (2 shorter events, 0.0 us)

commit v5 on v4

--- a/solution.py
+++ b/solution.py
@@ -1,3 +1,4 @@
+import functools
 import math
 
 import jax
@@ -40,8 +41,8 @@
     pl.semaphore_wait(barrier, len(devs))
 
 
-def attention_kernel(
-    len_ref, kv_ref, q_ref, wt_ref, x_ref, gain_ref, mark_ref, res_ref, normed_ref, table_ref,
+def attention_part(
+    weights, len_ref, kv_ref, q_ref, wt_ref, x_ref, gain_ref, mark_ref, res_ref, normed_ref, table_ref,
     marks, near, far, kbuf, vbuf, qbuf, wbuf, att, pbuf, rbuf,
     m_send, m_recv, n_send, n_recv, own_sem, kv_send, kv_recv, w_send, w_recv, sib_send, sib_recv, p_send, p_recv,
 ):
@@ -50,7 +51,12 @@
     peers = [(req, lax.rem(seq + i, 16)) for i in range(1, 16)]
     chips = [(lax.rem(m + i, 16) * 2 + c, seq) for i in range(1, 16)]
     sibling = (m * 2 + 1 - c, seq)
-    greet(peers + chips + [sibling])
+    x, y, z, _ = coords()
+    across = [device(lax.rem(x + i, 4), y, z, 1 - c) for i in range(1, 4)]
+    along = [device(x, y, lax.rem(z + i, 8), c) for i in range(1, 8)]
+    greet(peers + chips + [sibling] + across + along)
+    for copy in weights:
+        copy.start()
 
     def piece(part, dst_seq, src_seq, i):
         rows = pl.ds(pl.multiple_of(src_seq * 128, 128), 128)
@@ -193,39 +199,6 @@
     r = residual.astype(F32)
     mean = jnp.mean(r * r, axis=-1, keepdims=True)
     normed_ref[...] = (r * lax.rsqrt(mean + EPS) * gain_ref[...]).astype(BF)
-
-
-def attention(cached_len, kv, q, wt, x, gain, mark):
-    vm = pl.BlockSpec(memory_space=pltpu.VMEM)
-    dma = pltpu.SemaphoreType.DMA
-    return pl.pallas_call(
-        attention_kernel,
-        name="attention",
-        out_shape=[jax.ShapeDtypeStruct((16, D), BF)] * 2
-        + [jax.ShapeDtypeStruct((8, 16, 128), F32)],
-        in_specs=[pl.BlockSpec(memory_space=pltpu.SMEM)] + [vm] * 6,
-        out_specs=[vm] * 3,
-        scratch_shapes=[
-            pltpu.VMEM((16, 16, 128), F32),
-            pltpu.VMEM((8, 16, 128), F32),
-            pltpu.VMEM((4, 8, 16, 128), F32),
-            pltpu.VMEM((2048, HD), BF),
-            pltpu.VMEM((2048, HD), BF),
-            pltpu.VMEM((256, 256), BF),
-            pltpu.VMEM((16, 2, 64, 256), BF),
-            pltpu.VMEM((256, 256), BF),
-            pltpu.VMEM((256, D), BF),
-            pltpu.VMEM((16, 16, D), BF),
-            dma((16,)), dma((16,)),
-            dma((4,)), dma((4,)),
-            dma((5,)),
-            dma((3, 16)), dma((3, 16)),
-            dma((16,)), dma((16,)),
-            dma, dma,
-            dma((16,)), dma((16,)),
-        ],
-        compiler_params=pltpu.CompilerParams(collective_id=0, has_side_effects=True),
-    )(cached_len, kv, q, wt, x, gain, mark)
 
 
 ORDER = (0, 1, 7, 2, 6, 3, 5, 4)
@@ -300,8 +273,8 @@
 )
 
 
-def experts_kernel(
-    normed_ref, res_ref, table_ref, wg_ref, wd_ref, out_ref,
+def experts_part(
+    weights, normed_ref, res_ref, table_ref, wg_ref, wd_ref, out_ref,
     tok, comb, xs, xr, po, pr, part, sl, rl, sr, rr, fs, fr,
     z_send, z_recv, y_send, y_recv, x_send, x_recv, b_send, b_recv, r_send, r_recv, f_send, f_recv,
 ):
@@ -315,8 +288,6 @@
 
     def at_z(i):
         return device(x, y, lax.rem(z + i, 8), c)
-
-    greet([at_z(i) for i in range(1, 8)] + [right, left] + [at_x(j) for j in range(1, 8)])
 
     where_z = {r: (ch, zz) for ch, rs in enumerate(CHUNKS) for zz, r in enumerate(rs)}
 
@@ -489,6 +460,8 @@
         z_copy(r).start()
     tok[0, 0, :16] = normed_ref[...]
 
+    for copy in weights:
+        copy.wait()
     work = {"g": gather, "s": select, "f": feed, "c": combine, "r": scatter, "n": lambda ch, _: finish(ch)}
     for kind, ch, i in PLAN:
         work[kind](ch, i)
@@ -519,18 +492,49 @@
     lax.fori_loop(0, 8, sent, 0)
 
 
-def experts(normed, residual, table, wg, wd):
+def layer_kernel(counts, *refs):
+    groups, at = [], 0
+    for n in counts:
+        groups.append(refs[at : at + n])
+        at += n
+    ins, (wg_hbm, wd_hbm, out_ref), middle, (wg, wd, w_sem), first, second = groups
+    weights = [
+        pltpu.make_async_copy(wg_hbm, wg, w_sem.at[0]),
+        pltpu.make_async_copy(wd_hbm, wd, w_sem.at[1]),
+    ]
+    res, normed, table = middle
+    attention_part(weights, *ins, res, normed, table, *first)
+    experts_part(weights, normed, res, table, wg, wd, out_ref, *second)
+
+
+def layer(cached_len, kv, q, wt, x, gain, mark, wg, wd):
     vm = pl.BlockSpec(memory_space=pltpu.VMEM)
+    anywhere = pl.BlockSpec(memory_space=pl.ANY)
     dma = pltpu.SemaphoreType.DMA
     big = pltpu.VMEM((8, 8, 16, D), BF)
     hop = pltpu.VMEM((4, 4, 32, D), BF)
-    return pl.pallas_call(
-        experts_kernel,
-        name="experts",
-        out_shape=jax.ShapeDtypeStruct((16, D), BF),
-        in_specs=[vm] * 5,
-        out_specs=vm,
-        scratch_shapes=[
+    middle = [pltpu.VMEM((16, D), BF), pltpu.VMEM((16, D), BF), pltpu.VMEM((8, 16, 128), F32)]
+    held = [pltpu.VMEM(wg.shape, BF), pltpu.VMEM(wd.shape, BF), dma((2,))]
+    first = [
+            pltpu.VMEM((16, 16, 128), F32),
+            pltpu.VMEM((8, 16, 128), F32),
+            pltpu.VMEM((4, 8, 16, 128), F32),
+            pltpu.VMEM((2048, HD), BF),
+            pltpu.VMEM((2048, HD), BF),
+            pltpu.VMEM((256, 256), BF),
+            pltpu.VMEM((16, 2, 64, 256), BF),
+            pltpu.VMEM((256, 256), BF),
+            pltpu.VMEM((256, D), BF),
+            pltpu.VMEM((16, 16, D), BF),
+            dma((16,)), dma((16,)),
+            dma((4,)), dma((4,)),
+            dma((5,)),
+            dma((3, 16)), dma((3, 16)),
+            dma((16,)), dma((16,)),
+            dma, dma,
+            dma((16,)), dma((16,)),
+    ]
+    second = [
             pltpu.VMEM((4, 8, 32, D), BF),
             pltpu.VMEM((8, 128, 128), BF),
             big, big, big, big,
@@ -544,11 +548,19 @@
             dma((8, 8)), dma((8, 8)),
             dma((2, 4, 4)), dma((2, 4, 4)),
             dma((8,)), dma((8,)),
-        ],
+    ]
+    counts = (7, 3, 3, 3, len(first), len(second))
+    return pl.pallas_call(
+        functools.partial(layer_kernel, counts),
+        name="layer",
+        out_shape=jax.ShapeDtypeStruct((16, D), BF),
+        in_specs=[pl.BlockSpec(memory_space=pltpu.SMEM)] + [vm] * 6 + [anywhere] * 2,
+        out_specs=vm,
+        scratch_shapes=middle + held + first + second,
         compiler_params=pltpu.CompilerParams(
-            collective_id=1, has_side_effects=True, vmem_limit_bytes=56 * 1024 * 1024
+            collective_id=0, has_side_effects=True, vmem_limit_bytes=60 * 1024 * 1024
         ),
-    )(normed, residual, table, wg, wd)
+    )(cached_len, kv, q, wt, x, gain, mark, wg, wd)
 
 
 def local(
@@ -559,10 +571,11 @@
     mark = jnp.concatenate([routes[0].T.astype(F32), route_gates[0].T], 0)
     mark = jnp.where(jnp.arange(128)[None] // 16 == z, jnp.tile(mark, (1, 8)), 0.0)
     kv = jnp.concatenate([cache_kv[0], fresh_kv[0]], 0)
-    residual, normed, table = attention(
-        cached_len, kv, queries[0], out_weight.T, layer_input[0], norm_gain[None], mark
+    out = layer(
+        cached_len, kv, queries[0], out_weight.T, layer_input[0], norm_gain[None], mark,
+        w_gate_up[0], w_down[0],
     )
-    return experts(normed, residual, table, w_gate_up[0], w_down[0])[None]
+    return out[None]
 
 
 def solution(mesh):

time: 225 us -> 222 us (0.987)
  Pallas kernels: 217 us -> 213 us
    pallas_call x2 -> x1, Pallas kernels: 217 us -> 213 us  [layer(): pl.pallas_call(functools.partial(layer_kernel, counts), name='layer', out...]
where the time goes in v5:
time: 222 us; the launch traced here: 219 us
  Pallas kernels  213 us (96%)
  other arithmetic  3.66 us (2%)
    pallas_call x1, Pallas kernels, layer(): pl.pallas_call(functools.partial(layer_kernel, counts), name='layer', out...  213 us

profile of v5, /device:TPU:6, one launch (start us, length us, event | category | flops | bytes accessed | tf_op | source)
XLA Modules:
  0.0 219.1 jit_solution(4085546712647045854)
XLA Ops:
  0.7 0.7 convert_bitcast_fusion
  1.4 0.7 pad_maximum_fusion.1
  2.1 0.1 tile.10
  2.1 0.6 broadcast_select_fusion.refs_6_
  2.7 1.7 pad_maximum_fusion.refs_1_
  4.4 213.2 %layer.1 = bf16[16,2048]{1,0:T(8,128)(2,1)} custom-call(s32[1]{0:T(128)S(6)} %copy.13.refs_0_, bf16[128,1024]{1,0:T(8,128)(2,1)} %pad_maximum_fusion.refs_1_, bf16[16,4096]{1,0:T(8,128)(2,1)} %bitcast.20, bf16[64,256]{1,0:T(8,128)(2,1)} %bitcast.22, bf16[16,2048]{1,0:T(8,128)(2,1)} %bitcast.21, f32[1,2048]{1,0:T(1,128)} %bitcast.24, ...), custom_call_target="tpu_custom_call" | custom-call | tf_op jit(solution)/shard_map/layer/pallas_call | solution.py:553
  217.6 1.5 copy.14
  (2 shorter events, 0.0 us)

commit v6 on v5

--- a/solution.py
+++ b/solution.py
@@ -42,8 +42,8 @@
 
 
 def attention_part(
-    weights, len_ref, kv_ref, q_ref, wt_ref, x_ref, gain_ref, mark_ref, res_ref, normed_ref, table_ref,
-    marks, near, far, kbuf, vbuf, qbuf, wbuf, att, pbuf, rbuf,
+    weights, len_ref, kv_ref, q_ref, wt_ref, x_ref, gain_ref, routes_ref, gates_ref, res_ref, normed_ref, table_ref,
+    mark_ref, marks, near, far, kbuf, vbuf, qbuf, wbuf, att, pbuf, rbuf,
     m_send, m_recv, n_send, n_recv, own_sem, kv_send, kv_recv, w_send, w_recv, sib_send, sib_recv, p_send, p_recv,
 ):
     req, seq = lax.axis_index("req"), lax.axis_index("seq")
@@ -52,6 +52,11 @@
     chips = [(lax.rem(m + i, 16) * 2 + c, seq) for i in range(1, 16)]
     sibling = (m * 2 + 1 - c, seq)
     x, y, z, _ = coords()
+    row = lax.broadcasted_iota(jnp.int32, (16, 128), 0)
+    place = lax.broadcasted_iota(jnp.int32, (16, 128), 1) == row + z * 16
+    place = jnp.where(place, 1.0, 0.0).astype(BF)
+    both = jnp.concatenate([routes_ref[...].astype(F32), gates_ref[...]], 0).astype(BF)
+    mark_ref[...] = jnp.dot(both, place, preferred_element_type=F32)
     across = [device(lax.rem(x + i, 4), y, z, 1 - c) for i in range(1, 4)]
     along = [device(x, y, lax.rem(z + i, 8), c) for i in range(1, 8)]
     greet(peers + chips + [sibling] + across + along)
@@ -507,7 +512,7 @@
     experts_part(weights, normed, res, table, wg, wd, out_ref, *second)
 
 
-def layer(cached_len, kv, q, wt, x, gain, mark, wg, wd):
+def layer(cached_len, kv, q, wt, x, gain, routes, gates, wg, wd):
     vm = pl.BlockSpec(memory_space=pltpu.VMEM)
     anywhere = pl.BlockSpec(memory_space=pl.ANY)
     dma = pltpu.SemaphoreType.DMA
@@ -516,6 +521,7 @@
     middle = [pltpu.VMEM((16, D), BF), pltpu.VMEM((16, D), BF), pltpu.VMEM((8, 16, 128), F32)]
     held = [pltpu.VMEM(wg.shape, BF), pltpu.VMEM(wd.shape, BF), dma((2,))]
     first = [
+            pltpu.VMEM((16, 128), F32),
             pltpu.VMEM((16, 16, 128), F32),
             pltpu.VMEM((8, 16, 128), F32),
             pltpu.VMEM((4, 8, 16, 128), F32),
@@ -549,31 +555,28 @@
             dma((2, 4, 4)), dma((2, 4, 4)),
             dma((8,)), dma((8,)),
     ]
-    counts = (7, 3, 3, 3, len(first), len(second))
+    counts = (8, 3, 3, 3, len(first), len(second))
     return pl.pallas_call(
         functools.partial(layer_kernel, counts),
         name="layer",
         out_shape=jax.ShapeDtypeStruct((16, D), BF),
-        in_specs=[pl.BlockSpec(memory_space=pltpu.SMEM)] + [vm] * 6 + [anywhere] * 2,
+        in_specs=[pl.BlockSpec(memory_space=pltpu.SMEM)] + [vm] * 7 + [anywhere] * 2,
         out_specs=vm,
         scratch_shapes=middle + held + first + second,
         compiler_params=pltpu.CompilerParams(
             collective_id=0, has_side_effects=True, vmem_limit_bytes=60 * 1024 * 1024
         ),
-    )(cached_len, kv, q, wt, x, gain, mark, wg, wd)
+    )(cached_len, kv, q, wt, x, gain, routes, gates, wg, wd)
 
 
 def local(
     layer_input, queries, fresh_kv, cache_kv, cached_len, out_weight, norm_gain,
     routes, route_gates, w_gate_up, w_down,
 ):
-    z = coords()[2]
-    mark = jnp.concatenate([routes[0].T.astype(F32), route_gates[0].T], 0)
-    mark = jnp.where(jnp.arange(128)[None] // 16 == z, jnp.tile(mark, (1, 8)), 0.0)
     kv = jnp.concatenate([cache_kv[0], fresh_kv[0]], 0)
     out = layer(
-        cached_len, kv, queries[0], out_weight.T, layer_input[0], norm_gain[None], mark,
-        w_gate_up[0], w_down[0],
+        cached_len, kv, queries[0], out_weight.T, layer_input[0], norm_gain[None],
+        routes[0].T, route_gates[0].T, w_gate_up[0], w_down[0],
     )
     return out[None]
 

time: 222 us -> 220 us (level)
  no operation moved by 1% of the time
where the time goes in v6:
time: 220 us; the launch traced here: 216 us
  Pallas kernels  212 us (96%)
    pallas_call x1, Pallas kernels, layer(): pl.pallas_call(functools.partial(layer_kernel, counts), name='layer', out...  212 us

profile of v6, /device:TPU:6, one launch (start us, length us, event | category | flops | bytes accessed | tf_op | source)
XLA Modules:
  0.0 216.3 jit_solution(362965494066139692)
XLA Ops:
  0.7 1.7 pad_maximum_fusion.refs_1_
  2.3 212.5 %layer.1 = bf16[16,2048]{1,0:T(8,128)(2,1)} custom-call(s32[1]{0:T(128)S(6)} %copy.13.refs_0_, bf16[128,1024]{1,0:T(8,128)(2,1)} %pad_maximum_fusion.refs_1_, bf16[16,4096]{1,0:T(8,128)(2,1)} %bitcast.19, bf16[64,256]{1,0:T(8,128)(2,1)} %bitcast.21, bf16[16,2048]{1,0:T(8,128)(2,1)} %bitcast.20, f32[1,2048]{1,0:T(1,128)} %bitcast.23, s32[8,16]{1,0:T(8,128)} %bitcast.24, ...), custom_call_target="tpu_custom_call" | custom-call | tf_op jit(solution)/shard_map/layer/pallas_call | solution.py:559
  214.8 1.5 copy.14
